TPU v7x, 256 devices: a whole 4x4x8 slice. The times are simulated.
256 devices in a mesh: dp: 16 (over y, x), seq: 16 (over z, core).
Axes of the slice: x: 4, y: 4, z: 8, core: 2. Of those that a mesh axis runs over, the one named last changes fastest.
Arguments:
- ssm_input: bfloat16 [16, 2048, 2048], P('dp', 'seq'), may hold values from -6 to 6
- gate_input: bfloat16 [16, 2048, 2048], P('dp', 'seq'), may hold values from -6 to 6
- grad_gated: bfloat16 [16, 2048, 2048], P('dp', 'seq'), may hold values from -6 to 6
- x_proj: bfloat16 [2048, 96], replicated, may hold values from -0.125 to 0.125
- dt_proj: bfloat16 [64, 2048], replicated, may hold values from -0.75 to 0.75
- dt_bias: float32 [2048], replicated, may hold values from -14 to -2
- fid_bias: float32 [2, 2048], replicated, may hold values from -3 to 3
- a_log: float32 [2048, 16], replicated, may hold values from 0 to 2.77
- skip_gain: float32 [2048], replicated, may hold values from 0.5 to 1.5
- rec_lengths: int32 [16], P('dp'), may hold values from 512 to 2048, as said below
- fid_labels: int32 [16], P('dp'), may hold values from 0 to 1
Outputs:
- gated: bfloat16 [16, 2048, 2048], P('dp', 'seq')
- grad_input: bfloat16 [16, 2048, 2048], P('dp', 'seq')
- grad_gate: bfloat16 [16, 2048, 2048], P('dp', 'seq')
- grad_x_proj: float32 [2048, 96], P('dp')
- grad_dt_proj: float32 [64, 2048], P(None, 'dp')
- grad_a_log: float32 [2048, 16], P('dp')
- grad_skip: float32 [2048], P('dp')
- grad_dt_bias: float32 [2048], P('dp')
- grad_fid_bias: float32 [2, 2048], P(None, 'dp')
Inputs may be any that keep to these rules, and one draw needn't show every extreme that they name: `rec_lengths`: each record's count of valid time steps; in every draw some record is 2048 long.
All inputs are finite; a program needn't handle non-finite values.
Results may differ from a plain program's by a relative error of at most 0.0068.
Values sent between devices are 32-bit elements; how exact they have to be, the bound alone decides.
A program may use at most 64 MiB of HBM per device.

v0:
```python
import jax
import jax.numpy as jnp
from jax import lax
from jax.sharding import PartitionSpec as P


def passed_along(block, axis, distance):
    devices = range(lax.axis_size(axis))
    route = [(i - distance, i) for i in devices if i - distance in devices]
    return lax.ppermute(block, axis, route)


def run_block(h_now, a_trans, pieces):
    step_blk, b_blk, c_blk, val_blk = pieces
    outputs = []
    for position in range(step_blk.shape[0]):
        decay = jnp.exp(a_trans * step_blk[position][None, :])
        h_now = (
            decay * h_now
            + b_blk[position][:, None] * (step_blk[position] * val_blk[position])[None, :]
        )
        outputs.append(jnp.sum(c_blk[position][:, None] * h_now, axis=0))
    return (h_now, jnp.stack(outputs))


def to_blocks(array, turns):
    return array.reshape((turns, array.shape[0] // turns) + array.shape[1:])


def forward_record(h_start, a_trans, pieces, turns):
    blocks = tuple((to_blocks(piece, turns) for piece in pieces))

    def advance(h_now, blk_pieces):
        h_next, outputs = run_block(h_now, a_trans, blk_pieces)
        return (h_next, (h_now, outputs))

    h_last, (checks, outputs) = lax.scan(advance, h_start, blocks)
    return (h_last, checks, outputs.reshape((-1, outputs.shape[-1])))


def pull_record(stepsize, c_proj, y_grad, a_trans, turns):
    blocks = (to_blocks(stepsize, turns), to_blocks(c_proj, turns), to_blocks(y_grad, turns))

    def pull_retreat(adjoint, blk_pieces):
        step_blk, c_blk, grad_blk = blk_pieces
        for position in range(step_blk.shape[0] - 1, -1, -1):
            gathered = c_blk[position][:, None] * grad_blk[position][None, :] + adjoint
            adjoint = jnp.exp(a_trans * step_blk[position][None, :]) * gathered
        return (adjoint, None)

    adjoint, _ = lax.scan(pull_retreat, jnp.zeros_like(a_trans), blocks, reverse=True)
    return adjoint


def backward_record(checks, end_grad, a_trans, pieces, y_grad, turns):
    blocks = tuple((to_blocks(piece, turns) for piece in pieces))
    grad_blocks = to_blocks(y_grad, turns)

    def backward_retreat(carry, inputs):
        adjoint, a_total = carry
        h_in, blk_pieces, grad_blk = inputs
        _, block_back = jax.vjp(run_block, h_in, a_trans, blk_pieces)
        h_grad, a_part, piece_grads = block_back((adjoint, grad_blk))
        return ((h_grad, a_total + a_part), piece_grads)

    (_, a_grad), piece_grads = lax.scan(
        backward_retreat,
        (end_grad, jnp.zeros_like(a_trans)),
        (checks, blocks, grad_blocks),
        reverse=True,
    )
    flat = tuple((grad.reshape((-1,) + grad.shape[2:]) for grad in piece_grads))
    return flat + (a_grad,)


def per_device(
    ssm_input,
    gate_input,
    grad_gated,
    x_proj,
    dt_proj,
    dt_bias,
    fid_bias,
    a_log,
    skip_gain,
    rec_lengths,
    fid_labels,
):
    records, seg_len, channels = ssm_input.shape
    low_rank = dt_proj.shape[0]
    states = a_log.shape[1]
    fidelities = fid_bias.shape[0]
    turns = min(16, seg_len)
    projected = jnp.einsum("rle,ek->rlk", ssm_input, x_proj, preferred_element_type=jnp.float32)
    low = projected[:, :, :low_rank].astype(jnp.bfloat16)
    b_proj = projected[:, :, low_rank : low_rank + states]
    c_proj = projected[:, :, low_rank + states :]
    onehot = (fid_labels[:, None] == jnp.arange(fidelities, dtype=jnp.int32)[None, :]).astype(
        jnp.float32
    )
    fid_shift = jnp.dot(onehot, fid_bias, precision=lax.Precision.HIGHEST)
    dt_raw = (
        jnp.einsum("rlk,ke->rle", low, dt_proj, preferred_element_type=jnp.float32)
        + dt_bias
        + fid_shift[:, None, :]
    )
    positions = lax.axis_index("seq") * seg_len + jnp.arange(seg_len, dtype=jnp.int32)
    live = (positions[None, :] < rec_lengths[:, None]).astype(jnp.float32)[:, :, None]
    stepsize = jax.nn.softplus(dt_raw) * live
    a_matrix = -jnp.exp(a_log)
    a_trans = a_matrix.T
    values = ssm_input.astype(jnp.float32)
    s_total = jnp.sum(stepsize, axis=1)

    def zero_ends(pieces):
        h_last, _, _ = forward_record(jnp.zeros_like(a_trans), a_trans, pieces, turns)
        return h_last

    h_end = lax.map(zero_ends, (stepsize, b_proj, c_proj, values))
    gate_value = gate_input.astype(jnp.float32)
    gate_sigmoid = jax.nn.sigmoid(gate_value)
    gate_silu = gate_value * gate_sigmoid
    out_grad = grad_gated.astype(jnp.float32) * live
    y_grad = out_grad * gate_silu

    def pulls(pieces):
        step_rec, c_rec, grad_rec = pieces
        return pull_record(step_rec, c_rec, grad_rec, a_trans, turns)

    h_pull = lax.map(pulls, (stepsize, c_proj, y_grad))
    decay_total = jnp.exp(a_trans[None] * s_total[:, None, :])

    def forward_turn(turn, incoming):
        return passed_along(decay_total * incoming + h_end, "seq", 1)

    def backward_turn(turn, incoming):
        return passed_along(h_pull + decay_total * incoming, "seq", -1)

    h_start = lax.fori_loop(0, lax.axis_size("seq") - 1, forward_turn, jnp.zeros_like(h_end))
    end_grad = lax.fori_loop(0, lax.axis_size("seq") - 1, backward_turn, jnp.zeros_like(h_pull))

    def full_forward(pieces):
        start_rec, step_rec, b_rec, c_rec, val_rec = pieces
        _, checks, outputs = forward_record(
            start_rec, a_trans, (step_rec, b_rec, c_rec, val_rec), turns
        )
        return (checks, outputs)

    checks, y_ssm = lax.map(full_forward, (h_start, stepsize, b_proj, c_proj, values))
    y_full = y_ssm + skip_gain * values
    gated = (y_full * gate_silu * live).astype(jnp.bfloat16)
    grad_gate = (
        out_grad * y_full * (gate_sigmoid * (1.0 + gate_value * (1.0 - gate_sigmoid)))
    ).astype(jnp.bfloat16)

    def full_backward(pieces):
        check_rec, end_rec, step_rec, b_rec, c_rec, val_rec, grad_rec = pieces
        return backward_record(
            check_rec, end_rec, a_trans, (step_rec, b_rec, c_rec, val_rec), grad_rec, turns
        )

    step_grad, b_grad, c_grad, u_grad, a_grads = lax.map(
        full_backward, (checks, end_grad, stepsize, b_proj, c_proj, values, y_grad)
    )
    a_grad = jnp.sum(a_grads, axis=0).T
    dt_grad = step_grad * live * jax.nn.sigmoid(dt_raw)
    dt_grad_b = dt_grad.astype(jnp.bfloat16)
    dt_proj_part = jnp.einsum("rlk,rle->ek", low, dt_grad_b, preferred_element_type=jnp.float32)
    low_grad = jnp.einsum("rle,ke->rlk", dt_grad_b, dt_proj, preferred_element_type=jnp.float32)
    proj_grad = jnp.concatenate([low_grad, b_grad, c_grad], axis=2).astype(jnp.bfloat16)
    x_proj_part = jnp.einsum(
        "rle,rlk->ek", ssm_input, proj_grad, preferred_element_type=jnp.float32
    )
    input_grad = (
        u_grad
        + y_grad * skip_gain
        + jnp.einsum("rlk,ek->rle", proj_grad, x_proj, preferred_element_type=jnp.float32)
    )
    grad_input = input_grad.astype(jnp.bfloat16)
    dt_sums = jnp.sum(dt_grad, axis=1)
    packed = jnp.concatenate(
        [
            x_proj_part,
            dt_proj_part,
            a_grad * a_matrix,
            jnp.sum(y_grad * values, axis=(0, 1))[:, None],
            jnp.sum(dt_sums, axis=0)[:, None],
            jnp.dot(dt_sums.T, onehot, precision=lax.Precision.HIGHEST),
        ],
        axis=1,
    )
    totals = lax.psum(packed, "seq")
    shares = lax.psum_scatter(totals, "dp", scatter_dimension=0, tiled=True)
    col_x = low_rank + 2 * states
    col_dt = col_x + low_rank
    col_a = col_dt + states
    grad_x_proj = shares[:, :col_x]
    grad_dt_proj = shares[:, col_x:col_dt].T
    grad_a_log = shares[:, col_dt:col_a]
    grad_skip = shares[:, col_a]
    grad_dt_bias = shares[:, col_a + 1]
    grad_fid_bias = shares[:, col_a + 2 :].T
    return (
        gated,
        grad_input,
        grad_gate,
        grad_x_proj,
        grad_dt_proj,
        grad_a_log,
        grad_skip,
        grad_dt_bias,
        grad_fid_bias,
    )


def solution(mesh):
    in_specs = (
        P("dp", "seq", None),
        P("dp", "seq", None),
        P("dp", "seq", None),
        P(),
        P(),
        P(),
        P(),
        P(),
        P(),
        P("dp"),
        P("dp"),
    )
    out_specs = (
        P("dp", "seq", None),
        P("dp", "seq", None),
        P("dp", "seq", None),
        P("dp", None),
        P(None, "dp"),
        P("dp", None),
        P("dp"),
        P("dp"),
        P(None, "dp"),
    )
    return jax.shard_map(
        per_device, mesh=mesh, in_specs=in_specs, out_specs=out_specs, check_vma=False
    )
```

profile of v0, /device:TPU:1, one launch (start us, length us, event | category | flops | bytes accessed | tf_op | source)
XLA Modules:
  0.0 812.1 jit_solution(1618265109441323945)
XLA Ops:
  14.2 38.7 %while.126 = (s32[]{:T(128)}, f32[16,2048]{1,0:T(8,128)S(1)}, f32[16,8,2048]{2,1,0:T(8,128)}, f32[16,2048]{1,0:T(8,128)S(1)}, f32[16,8,16]{2,1,0:T(8,128)}, /*in...) while((s32[]{:T(128)}, f32[16,2048]{1,0:T(8,128)S(1)}, ...), condition=%wide.region_2.3_spmd.clone, body=%wide.region_1.2_spmd.clone.sunk | while | flops 1097738 | bytes 985871 | solution.py:37
  54.0 95.3 %while.123 = (s32[]{:T(128)}, f32[1,16,2048]{2,1,0:T(8,128)S(1)}, f32[1,16,2048]{2,1,0:T(8,128)S(1)}, f32[1,16,2048]{2,1,0:T(8,128)S(1)}, s32[]{:T(128)}) while((s32[]{:T(128)}, f32[1,16,2048]{2,1,0:T(8,128)S(1)}, f32[1,16,2048]{2,1,0:T(8,128)S(1)}, f32[1,16,2048]{2,1,0:T(8,128)S(1)}, s32[]{:T(128)}) %tuple.429), condition=%wide.region_4.5_spmd, body=%wide.region_3.4_spmd.sunk | while | flops 65538 | bytes 1048677 | solution.py:139
  54.0 4.9 collective-permute-start
  60.9 4.4 collective-permute-start
  67.2 4.4 collective-permute-start
  73.5 4.4 collective-permute-start
  79.8 4.4 collective-permute-start
  86.2 4.4 collective-permute-start
  92.5 4.4 collective-permute-start
  98.8 4.4 collective-permute-start
  105.1 4.4 collective-permute-start
  150.3 73.6 %while.124 = (s32[]{:T(128)}, f32[16,2048]{1,0:T(8,128)S(1)}, f32[16,16,2048]{2,1,0:T(8,128)}, f32[16,8,2048]{2,1,0:T(8,128)}, f32[16,8,2048]{2,1,0:T(8,128)}, /...) while((s32[]{:T(128)}, f32[16,2048]{1,0:T(8,128)S(1)}, ...), condition=%wide.region_14.15_spmd, body=%wide.region_5.0_spmd.sunk | while | flops 2359305 | bytes 2333341 | solution.py:37
  228.0 70.4 %while.127 = (s32[]{:T(128)}, f32[16,2048]{1,0:T(8,128)S(1)}, f32[16,8,2048]{2,1,0:T(8,128)}, f32[16,2048]{1,0:T(8,128)S(1)}, f32[16,8,16]{2,1,0:T(8,128)}, /*in...) while((s32[]{:T(128)}, f32[16,2048]{1,0:T(8,128)S(1)}, ...), condition=%wide.region_16.17_spmd.clone, body=%wide.region_15.16_spmd.clone.sunk | while | flops 1081355 | bytes 789283 | solution.py:51
  299.4 114.7 %while.125 = (s32[]{:T(128)}, f32[1,16,2048]{2,1,0:T(8,128)S(1)}, f32[1,16,2048]{2,1,0:T(8,128)S(1)}, f32[1,16,2048]{2,1,0:T(8,128)S(1)}, s32[]{:T(128)}) while((s32[]{:T(128)}, f32[1,16,2048]{2,1,0:T(8,128)S(1)}, f32[1,16,2048]{2,1,0:T(8,128)S(1)}, f32[1,16,2048]{2,1,0:T(8,128)S(1)}, s32[]{:T(128)}) %tuple.428), condition=%wide.region_18.19_spmd, body=%wide.region_17.18_spmd.sunk | while | flops 65538 | bytes 1048677 | solution.py:140
  301.4 5.7 collective-permute-done.1
  309.1 5.4 collective-permute-done.1
  316.5 6.3 collective-permute-done.1
  324.7 5.4 collective-permute-done.1
  332.1 6.3 collective-permute-done.1
  340.3 5.4 collective-permute-done.1
  347.7 6.3 collective-permute-done.1
  355.9 5.6 collective-permute-done.1
  363.5 5.6 collective-permute-done.1
  371.0 5.6 collective-permute-done.1
  378.5 5.6 collective-permute-done.1
  386.0 5.6 collective-permute-done.1
  393.6 5.6 collective-permute-done.1
  401.1 5.6 collective-permute-done.1
  408.6 5.6 collective-permute-done.1
  416.4 175.0 %while.128 = (s32[]{:T(128)}, f32[16,2048]{1,0:T(8,128)S(1)}, f32[16,2048]{1,0:T(8,128)S(1)}, f32[16,8,2048]{2,1,0:T(8,128)}, bf16[16,8,16]{2,1,0:T(8,128)(2,1)S...) while((s32[]{:T(128)}, f32[16,2048]{1,0:T(8,128)S(1)}, ...), condition=%wide.region_52.53_spmd.clone, body=%wide.region_19.52_spmd.clone.sunk | while | flops 8701451 | bytes 6086559 | solution.py:66
  598.1 93.7 %reduce-scatter.2.cloned.1.call-done = f32[128,180]{0,1:T(8,128)} async-done(((f32[2048,180]{0,1:T(8,128)}), f32[128,180]{0,1:T(8,128)}) %reduce-scatter.2.cloned.1.call-update) | async-done | bytes 92176 | tf_op jit(solution)/shard_map/reduce_scatter | solution.py:193
  694.3 104.4 %all-reduce.42.cloned.1.call-done = f32[128,180]{0,1:T(8,128)} async-done(((f32[128,180]{0,1:T(8,128)}), f32[128,180]{0,1:T(8,128)}) %all-reduce.42.cloned.1.call-update) | async-done | bytes 92176 | tf_op jit(solution)/shard_map/psum | solution.py:192
  (1209 shorter events, 467.1 us)
Async XLA Ops:
  7.2 684.6 %reduce-scatter.2.cloned.1.call-start = ((), (), s32[]{:S(2)}) async-start(), calls=%async_computation.1 | async-start | bytes 1601536 | tf_op jit(solution)/shard_map/reduce_scatter | solution.py:193
  54.0 6.9 collective-permute-start
  60.9 6.3 collective-permute-start
  67.2 6.3 collective-permute-start
  73.5 6.3 collective-permute-start
  79.8 6.3 collective-permute-start
  86.2 6.3 collective-permute-start
  92.5 6.3 collective-permute-start
  98.8 6.3 collective-permute-start
  105.1 6.3 collective-permute-start
  111.4 6.3 collective-permute-start
  117.7 6.3 collective-permute-start
  124.0 6.3 collective-permute-start
  130.3 6.3 collective-permute-start
  136.7 6.3 collective-permute-start
  143.0 6.3 collective-permute-start
  299.5 7.6 collective-permute-start.1
  307.1 7.4 collective-permute-start.1
  314.5 8.2 %collective-permute-start.1 = (f32[1,16,2048]{2,1,0:T(8,128)S(1)}, f32[1,16,2048]{2,1,0:T(8,128)S(1)}, u32[]{:S(2)}, u32[]{:S(2)}) collective-permute-start(f32[1,16,2048]{2,1,0:T(8,128)S(1)} %multiply_add_fusion.34), channel_id=1, source_target_pairs={{1,0},{2,1},{3,2},{4,3},{5,4},{6,5},{7,6},{8,7},{9,8},{10,9},{11,1... | collective-permute-start | bytes 393224 | tf_op jit(solution)/shard_map/while/body/eval_jaxpr/ppermute | solution.py:10
  322.8 7.4 collective-permute-start.1
  330.1 8.2 %collective-permute-start.1 = (f32[1,16,2048]{2,1,0:T(8,128)S(1)}, f32[1,16,2048]{2,1,0:T(8,128)S(1)}, u32[]{:S(2)}, u32[]{:S(2)}) collective-permute-start(f32[1,16,2048]{2,1,0:T(8,128)S(1)} %multiply_add_fusion.34), channel_id=1, source_target_pairs={{1,0},{2,1},{3,2},{4,3},{5,4},{6,5},{7,6},{8,7},{9,8},{10,9},{11,1... | collective-permute-start | bytes 393224 | tf_op jit(solution)/shard_map/while/body/eval_jaxpr/ppermute | solution.py:10
  338.4 7.4 collective-permute-start.1
  345.8 8.2 %collective-permute-start.1 = (f32[1,16,2048]{2,1,0:T(8,128)S(1)}, f32[1,16,2048]{2,1,0:T(8,128)S(1)}, u32[]{:S(2)}, u32[]{:S(2)}) collective-permute-start(f32[1,16,2048]{2,1,0:T(8,128)S(1)} %multiply_add_fusion.34), channel_id=1, source_target_pairs={{1,0},{2,1},{3,2},{4,3},{5,4},{6,5},{7,6},{8,7},{9,8},{10,9},{11,1... | collective-permute-start | bytes 393224 | tf_op jit(solution)/shard_map/while/body/eval_jaxpr/ppermute | solution.py:10
  354.0 7.5 collective-permute-start.1
  361.5 7.5 collective-permute-start.1
  369.1 7.5 collective-permute-start.1
  376.6 7.5 collective-permute-start.1
  384.1 7.5 collective-permute-start.1
  391.6 7.5 collective-permute-start.1
  399.1 7.5 collective-permute-start.1
  406.7 7.5 collective-permute-start.1
  598.0 200.6 %all-reduce.42.cloned.1.call-start = ((), (), s32[]{:S(2)}) async-start(), calls=%async_computation.2 | async-start | bytes 188416 | tf_op jit(solution)/shard_map/psum | solution.py:192
  (22 other events, 1057.0 us)
Sparse Core Ops, SparseCore 0:
  598.2 93.5 reduce-scatter.1
  694.1 104.5 all-reduce.41
where the time goes:
time: 823 us; the launch traced here: 812 us
  waiting for transfers between devices  312 us (38%)
  local copies, waits for them, and re-layouts  223 us (27%)
  other arithmetic  155 us (19%)
  starting transfers between devices  94.8 us (12%)
  between operations  15.8 us (2%)
    ppermute x30, waiting for transfers between devices, passed_along(): return lax.ppermute(block, axis, route)  114 us
    psum x1, waiting for transfers between devices, per_device(): totals = lax.psum(packed, 'seq')  104 us
    ppermute x30, starting transfers between devices, passed_along(): return lax.ppermute(block, axis, route)  94.7 us
    reduce_scatter x1, waiting for transfers between devices, per_device(): shares = lax.psum_scatter(totals, 'dp', scatter_dimension=0, tiled=True)  93.7 us
    slice x48, local copies, waits for them, and re-layouts, run_block(): val_blk[position]  69.5 us
    dynamic_slice x64, local copies, waits for them, and re-layouts, forward_record(): h_last, (checks, outputs) = lax.scan(advance, h_start, blocks)  44.5 us
    reduce_sum x80, other arithmetic, run_block(): outputs.append(jnp.sum(c_blk[position][:, None] * h_now, axis=0))  36.7 us
    reduce_sum x32, other arithmetic, run_block(): decay = jnp.exp(a_trans * step_blk[position][None, :])  33.4 us
  transfers between devices with their start and end apart: 32, of which 32 were waited for; matrix products, arithmetic and copies ran while one was open for 0% of the time, Pallas kernels for 0%

commit v1 on v0

v1 whole, which is shorter than its diff:
```python
import jax
import jax.numpy as jnp
from jax import lax
from jax.experimental import pallas as pl
from jax.experimental.pallas import tpu as pltpu
from jax.sharding import PartitionSpec as P

F32 = jnp.float32
BF16 = jnp.bfloat16
LOG2E = 1.4426950408889634
LN2 = 0.6931471805599453
T = 128
E = 2048
N = 16
RANK = 64
KT = E // 128
S = 8
L = T // S
COLS = RANK + 2 * N
ROWS = 192
HALF = ROWS // 2
MESH = pl.DeviceIdType.MESH
VMEM = pl.BlockSpec(memory_space=pltpu.VMEM)
SMEM = pl.BlockSpec(memory_space=pltpu.SMEM)


def lanes(k):
    return pl.ds(pl.multiple_of(k * 128, 128), 128)


def store_permuted(ref, k, value):
    for blk in range(T // 8):
        first = (blk % 2) * 64 + blk // 2
        ref[k, pl.ds(first, 8, stride=8), :] = value[blk * 8 : blk * 8 + 8, :]


def load_natural(ref, k):
    parts = []
    for blk in range(T // 8):
        first = (blk % 2) * 64 + blk // 2
        parts.append(ref[k, pl.ds(first, 8, stride=8), :])
    return jnp.concatenate(parts, axis=0)


def sigmoid(v):
    return 1.0 / (1.0 + jnp.exp(-v))


def softplus(v):
    z = jnp.exp(-jnp.abs(v))
    r = z / (z + 2.0)
    q = r * r
    poly = 1.0 / 15.0
    for odd in (13.0, 11.0, 9.0, 7.0, 5.0, 3.0, 1.0):
        poly = poly * q + 1.0 / odd
    return jnp.maximum(v, 0.0) + 2.0 * r * poly


def live_mask(len_ref):
    t0 = lax.axis_index("seq") * T
    pos = t0 + lax.broadcasted_iota(jnp.int32, (T, 128), 0)
    return (pos < len_ref[0]).astype(F32)


def fid_row(lab_ref, fid_ref, ls):
    label = lab_ref[0]
    row = jnp.zeros((1, 128), F32)
    for kind in range(2):
        row = row + jnp.where(label == kind, fid_ref[kind : kind + 1, ls], 0.0)
    return row


def row8(ref, n, ls):
    return jnp.broadcast_to(ref[n : n + 1, ls], (8, 128))


def phase_one(
    len_ref, lab_ref, u_ref, gate_ref, gg_ref, xp_ref, dtp_ref, dtb_ref, fid_ref, a2_ref,
    step_ref, su_ref, gy_ref, bb_ref, cb_ref, segs_ref, hs_ref, as_ref, send_ref, low_ref, a2w,
):
    proj = jnp.dot(u_ref[0], xp_ref[...], preferred_element_type=F32)
    low_ref[...] = proj[:, :RANK].astype(BF16)
    for n in range(N):
        for col, ref in ((RANK + n, bb_ref), (RANK + N + n, cb_ref)):
            wide = jnp.broadcast_to(proj[:, col : col + 1], (T, 128))
            for blk in range(T // 8):
                first = (blk % 2) * 8 * (N * S) + n * S + blk // 2
                ref[pl.ds(first, 8, stride=N * S), :] = wide[blk * 8 : blk * 8 + 8, :]
    live = live_mask(len_ref)

    @pl.loop(0, KT)
    def _(k):
        ls = lanes(k)
        dt_raw = (
            jnp.dot(low_ref[...], dtp_ref[:, ls], preferred_element_type=F32)
            + dtb_ref[:, ls]
            + fid_row(lab_ref, fid_ref, ls)
        )
        step = softplus(dt_raw) * live
        u = u_ref[0, :, ls].astype(F32)
        gate = gate_ref[0, :, ls].astype(F32)
        gy = gg_ref[0, :, ls].astype(F32) * live * (gate * sigmoid(gate))
        store_permuted(step_ref, k, step)
        store_permuted(su_ref, k, step * u)
        store_permuted(gy_ref, k, gy)
        for n in range(N):
            a2w[k, n * S : n * S + S, :] = row8(a2_ref, n, ls)

    GN, GK = 4, 2

    @pl.loop(0, KT // GK)
    def _(kp):
        @pl.loop(0, N // GN)
        def _(ng):
            ks = [kp * GK + i for i in range(GK)]
            ns = [ng * GN + i for i in range(GN)]
            a2 = [[a2w[k, pl.ds(pl.multiple_of(n * S, S), S), :] for k in ks] for n in ns]
            h = [[None] * GK for _ in ns]
            pr = [[None] * GK for _ in ns]
            acc = [[None] * GK for _ in ns]
            for tau in range(L):
                rows = pl.ds(tau * S, S)
                st = [step_ref[k, rows, :] for k in ks]
                su = [su_ref[k, rows, :] for k in ks]
                gy = [gy_ref[k, rows, :] for k in ks]
                for j, n in enumerate(ns):
                    at = pl.ds(pl.multiple_of(tau * N * S + n * S, S), S)
                    b = bb_ref[at, :]
                    c = cb_ref[at, :]
                    for i in range(GK):
                        d = jnp.exp2(a2[j][i] * st[i])
                        bs = b * su[i]
                        cg = c * gy[i]
                        if tau == 0:
                            h[j][i], pr[j][i] = bs, d
                            acc[j][i] = d * cg
                        else:
                            h[j][i] = d * h[j][i] + bs
                            pr[j][i] = pr[j][i] * d
                            acc[j][i] = acc[j][i] + pr[j][i] * cg
            for j, n in enumerate(ns):
                at = pl.ds(pl.multiple_of(n * S, S), S)
                for i, k in enumerate(ks):
                    hs_ref[k, at, :] = h[j][i]
                    as_ref[k, at, :] = acc[j][i]

    @pl.loop(0, KT)
    def _(k):
        seg = step_ref[k, pl.ds(0, S), :]
        for tau in range(1, L):
            seg = seg + step_ref[k, pl.ds(tau * S, S), :]
        segs_ref[k] = seg
        for nh in range(2):
            a2 = a2_ref[nh * 8 : nh * 8 + 8, lanes(k)]
            ps = [jnp.exp2(a2 * seg[s : s + 1, :]) for s in range(S)]
            h = hs_ref[k, pl.ds(nh * 64, 8, stride=8), :]
            for s in range(1, S):
                h = ps[s] * h + hs_ref[k, pl.ds(nh * 64 + s, 8, stride=8), :]
            g = as_ref[k, pl.ds(nh * 64 + S - 1, 8, stride=8), :]
            for s in range(S - 2, -1, -1):
                g = ps[s] * g + as_ref[k, pl.ds(nh * 64 + s, 8, stride=8), :]
            send_ref[k, pl.ds(nh * 8, 8), :] = h
            send_ref[k, pl.ds(16 + nh * 8, 8), :] = g
        total = jnp.sum(seg, axis=0, keepdims=True)
        send_ref[k, pl.ds(32, 8), :] = jnp.broadcast_to(total, (8, 128))


def exchange(send_ref, a2_ref, out_ref, got, back, ssem, rsem, ssem2, rsem2):
    size = lax.axis_size("seq")
    me = lax.axis_index("seq")
    barrier = pltpu.get_barrier_semaphore()
    for o in range(1, size):
        j = lax.rem(me + o, size)
        pl.semaphore_signal(barrier, inc=1, device_id={"seq": j}, device_id_type=MESH)
    pl.semaphore_wait(barrier, size - 1)

    def there(j, slot):
        return pltpu.make_async_remote_copy(
            src_ref=send_ref.at[j], dst_ref=got.at[slot], send_sem=ssem.at[j],
            recv_sem=rsem.at[slot], device_id={"seq": j}, device_id_type=MESH,
        )

    def home(j, slot):
        return pltpu.make_async_remote_copy(
            src_ref=back.at[j], dst_ref=out_ref.at[slot], send_sem=ssem2.at[j],
            recv_sem=rsem2.at[slot], device_id={"seq": j}, device_id_type=MESH,
        )

    for o in range(1, size):
        there(lax.rem(me + o, size), me).start()
    got[pl.ds(me, 1)] = send_ref[pl.ds(me, 1)]
    a2 = a2_ref[:, pl.ds(pl.multiple_of(me * 128, 128), 128)]
    for o in range(1, size):
        j = lax.rem(me + o, size)
        there(j, j).wait_recv()
    h = jnp.zeros((N, 128), F32)
    for i in range(size):
        back[i, 0:16, :] = h
        h = jnp.exp2(a2 * got[i, 32:33, :]) * h + got[i, 0:16, :]
    g = jnp.zeros((N, 128), F32)
    for i in range(size - 1, -1, -1):
        back[i, 16:32, :] = g
        g = jnp.exp2(a2 * got[i, 32:33, :]) * g + got[i, 16:32, :]
    for o in range(1, size):
        home(lax.rem(me + o, size), me).start()
    out_ref[pl.ds(me, 1)] = back[pl.ds(me, 1)]
    for o in range(1, size):
        j = lax.rem(me + o, size)
        home(j, j).wait_recv()
    for o in range(1, size):
        j = lax.rem(me + o, size)
        there(j, me).wait_send()
        home(j, me).wait_send()


def phase_two(
    len_ref, lab_ref, u_ref, gate_ref, gg_ref, xp_ref, dtp_ref, dtb_ref, fid_ref, a2_ref,
    skip_ref, step_ref, su_ref, gy_ref, bb_ref, cb_ref, segs_ref, hs_ref, as_ref, st_ref, low_ref,
    gated_ref, gin_ref, ggate_ref, grads_ref,
    hst, gst, hbuf, bgr, cgr, ybuf, sbuf, gbuf, agbuf, dtg, dirs,
):
    @pl.loop(0, KT)
    def _(k):
        for nh in range(2):
            a2 = a2_ref[nh * 8 : nh * 8 + 8, lanes(k)]
            ps = [jnp.exp2(a2 * segs_ref[k, s : s + 1, :]) for s in range(S)]
            h = st_ref[k, nh * 8 : nh * 8 + 8, :]
            for s in range(S):
                at = pl.ds(nh * 64 + s, 8, stride=8)
                hst[k, at, :] = h
                if s + 1 < S:
                    h = ps[s] * h + hs_ref[k, at, :]
            g = st_ref[k, 16 + nh * 8 : 24 + nh * 8, :]
            for s in range(S - 1, -1, -1):
                at = pl.ds(nh * 64 + s, 8, stride=8)
                gst[k, at, :] = g
                if s > 0:
                    g = ps[s] * g + as_ref[k, at, :]

    bgr[...] = jnp.zeros_like(bgr)
    cgr[...] = jnp.zeros_like(cgr)
    GK = 2

    @pl.loop(0, KT // GK)
    def _(kp):
        ks = [kp * GK + i for i in range(GK)]
        FN = 8
        for ng in range(N // FN):
            ns = [ng * FN + j for j in range(FN)]
            a2 = [[row8(a2_ref, n, lanes(k)) for k in ks] for n in ns]
            first = []
            for n in ns:
                for i, k in enumerate(ks):
                    h = hst[k, n * S : n * S + S, :]
                    hbuf[n * GK + i] = h
                    first.append(h)

            def ahead(tau, hh):
                rows = pl.ds(pl.multiple_of(tau * S, S), S)
                st = [step_ref[k, rows, :] for k in ks]
                su = [su_ref[k, rows, :] for k in ks]
                gy = [gy_ref[k, rows, :] for k in ks]
                ys = [None] * GK
                out = []
                for j, n in enumerate(ns):
                    at = pl.ds(pl.multiple_of(tau * (N * S) + n * S, S), S)
                    b = bb_ref[at, :]
                    c = cb_ref[at, :]
                    cg = None
                    for i in range(GK):
                        d = jnp.exp2(a2[j][i] * st[i])
                        h = d * hh[j * GK + i] + b * su[i]
                        out.append(h)
                        hbuf[(tau + 1) * (N * GK) + n * GK + i] = h
                        part = c * h
                        ys[i] = part if ys[i] is None else ys[i] + part
                        part = h * gy[i]
                        cg = part if cg is None else cg + part
                    cgr[at, :] = cgr[at, :] + cg
                for i, k in enumerate(ks):
                    if ng == 0:
                        ybuf[k, rows, :] = ys[i]
                    else:
                        ybuf[k, rows, :] = ybuf[k, rows, :] + ys[i]
                return tuple(out)

            lax.fori_loop(0, L, ahead, tuple(first))

        BN = 4
        for ng in range(N // BN):
            ns = [ng * BN + j for j in range(BN)]
            a2 = [[row8(a2_ref, n, lanes(k)) for k in ks] for n in ns]
            carry = []
            for n in ns:
                for k in ks:
                    carry.append(gst[k, n * S : n * S + S, :])
            zero = jnp.zeros((S, 128), F32)

            def behind(turn, state):
                tau = L - 1 - turn
                cs, ags = state
                rows = pl.ds(pl.multiple_of(tau * S, S), S)
                st = [step_ref[k, rows, :] for k in ks]
                su = [su_ref[k, rows, :] for k in ks]
                gy = [gy_ref[k, rows, :] for k in ks]
                sb = [None] * GK
                sg = [None] * GK
                new_c, new_a = [], []
                for j, n in enumerate(ns):
                    at = pl.ds(pl.multiple_of(tau * (N * S) + n * S, S), S)
                    b = bb_ref[at, :]
                    c = cb_ref[at, :]
                    bg = None
                    for i in range(GK):
                        d = jnp.exp2(a2[j][i] * st[i])
                        g = c * gy[i] + cs[j * GK + i]
                        part = g * b
                        sb[i] = part if sb[i] is None else sb[i] + part
                        part = g * su[i]
                        bg = part if bg is None else bg + part
                        dg = d * g
                        w = dg * hbuf[tau * (N * GK) + n * GK + i]
                        part = a2[j][i] * w
                        sg[i] = part if sg[i] is None else sg[i] + part
                        new_c.append(dg)
                        new_a.append(ags[j * GK + i] + st[i] * w)
                    bgr[at, :] = bgr[at, :] + bg
                for i, k in enumerate(ks):
                    if ng == 0:
                        sbuf[k, rows, :] = sb[i]
                        gbuf[k, rows, :] = sg[i]
                    else:
                        sbuf[k, rows, :] = sbuf[k, rows, :] + sb[i]
                        gbuf[k, rows, :] = gbuf[k, rows, :] + sg[i]
                return tuple(new_c), tuple(new_a)

            _, ags = lax.fori_loop(0, L, behind, (tuple(carry), (zero,) * (BN * GK)))
            for j, n in enumerate(ns):
                for i, k in enumerate(ks):
                    agbuf[k, n * S : n * S + S, :] = ags[j * GK + i]

    live = live_mask(len_ref)
    label = lab_ref[0]

    @pl.loop(0, KT)
    def _(k):
        ls = lanes(k)
        u = u_ref[0, :, ls].astype(F32)
        gate = gate_ref[0, :, ls].astype(F32)
        sig = sigmoid(gate)
        silu = gate * sig
        og = gg_ref[0, :, ls].astype(F32) * live
        y = load_natural(ybuf, k) + skip_ref[:, ls] * u
        gated_ref[0, :, ls] = (y * silu * live).astype(BF16)
        ggate_ref[0, :, ls] = (og * y * (sig * (1.0 + gate * (1.0 - sig)))).astype(BF16)
        dt_raw = (
            jnp.dot(low_ref[...], dtp_ref[:, ls], preferred_element_type=F32)
            + dtb_ref[:, ls]
            + fid_row(lab_ref, fid_ref, ls)
        )
        step_grad = LN2 * load_natural(gbuf, k) + u * load_natural(sbuf, k)
        dt_grad = step_grad * live * sigmoid(dt_raw)
        dt_b = dt_grad.astype(BF16)
        dtg[:, ls] = dt_b
        grads_ref[k, COLS : COLS + RANK, :] = lax.dot_general(
            low_ref[...], dt_b, (((0,), (0,)), ((), ())), preferred_element_type=F32
        )
        base = COLS + RANK
        for nh in range(2):
            ag = agbuf[k, pl.ds(nh * 64, 8, stride=8), :]
            for s in range(1, S):
                ag = ag + agbuf[k, pl.ds(nh * 64 + s, 8, stride=8), :]
            grads_ref[k, base + nh * 8 : base + nh * 8 + 8, :] = (
                ag * a2_ref[nh * 8 : nh * 8 + 8, ls] * LN2
            )
        skip_row = jnp.sum(og * silu * u, axis=0, keepdims=True)
        dt_row = jnp.sum(dt_grad, axis=0, keepdims=True)
        zero = jnp.zeros_like(dt_row)
        grads_ref[k, base + 16 : base + 24, :] = jnp.concatenate(
            [
                skip_row,
                dt_row,
                jnp.where(label == 0, dt_row, zero),
                jnp.where(label == 1, dt_row, zero),
                zero, zero, zero, zero,
            ],
            axis=0,
        )
        grads_ref[k, base + 24 : ROWS, :] = jnp.zeros((ROWS - base - 24, 128), F32)

    low_grad = lax.dot_general(
        dtg[...], dtp_ref[...], (((1,), (1,)), ((), ())), preferred_element_type=F32
    )
    lane = lax.broadcasted_iota(jnp.int32, (128, 128), 1)
    sums = jnp.zeros((T, 128), F32)
    for n in range(N):
        for col, ref in ((RANK + n, bgr), (RANK + N + n, cgr)):
            tile = jnp.concatenate([ref[tau * N * S + n * S : tau * N * S + n * S + S, :] for tau in range(L)], axis=0)
            hi = tile.astype(BF16)
            lo = (tile - hi.astype(F32)).astype(BF16)
            pick = (lane == col).astype(BF16)
            sums = sums + jnp.dot(hi, pick, preferred_element_type=F32)
            sums = sums + jnp.dot(lo, pick, preferred_element_type=F32)
    dirs[0] = sums
    sums = load_natural(dirs, 0)
    proj_grad = jnp.concatenate([low_grad, sums[:, RANK:COLS]], axis=1).astype(BF16)

    @pl.loop(0, KT)
    def _(k):
        ls = lanes(k)
        grads_ref[k, 0:COLS, :] = lax.dot_general(
            proj_grad, u_ref[0, :, ls], (((0,), (0,)), ((), ())), preferred_element_type=F32
        )
        back = lax.dot_general(
            proj_grad, xp_ref[ls, :], (((1,), (1,)), ((), ())), preferred_element_type=F32
        )
        direct = load_natural(step_ref, k) * load_natural(sbuf, k)
        gin_ref[0, :, ls] = (direct + load_natural(gy_ref, k) * skip_ref[:, ls] + back).astype(BF16)


def reduce_grads(g_ref, out_ref, pair, part, peers, mine, zparts, zsum, sems_a, sems_b, sems_c, sems_d):
    chips = lax.axis_size("dp")
    size = lax.axis_size("seq")
    depth = size // 2
    reducers = 6
    rows = HALF // reducers
    dp = lax.axis_index("dp")
    me = lax.axis_index("seq")
    z = me // 2
    core = lax.rem(me, 2)
    sib = me + 1 - 2 * core
    barrier = pltpu.get_barrier_semaphore()
    for o in range(1, chips):
        d = lax.rem(dp + o, chips)
        pl.semaphore_signal(barrier, inc=1, device_id={"dp": d}, device_id_type=MESH)
    for o in range(1, size):
        j = lax.rem(me + o, size)
        pl.semaphore_signal(barrier, inc=1, device_id={"seq": j}, device_id_type=MESH)
    pl.semaphore_wait(barrier, chips + size - 2)

    def to_sib(d):
        return pltpu.make_async_remote_copy(
            src_ref=g_ref.at[d, pl.ds(pl.multiple_of((1 - core) * HALF, 8), HALF)],
            dst_ref=pair.at[d], send_sem=sems_a.at[0, d], recv_sem=sems_a.at[1, d],
            device_id={"seq": sib}, device_id_type=MESH,
        )

    def to_chip(d, slot):
        return pltpu.make_async_remote_copy(
            src_ref=part.at[d], dst_ref=peers.at[slot], send_sem=sems_b.at[0, d],
            recv_sem=sems_b.at[1, slot], device_id={"dp": d}, device_id_type=MESH,
        )

    def to_level(r, slot):
        return pltpu.make_async_remote_copy(
            src_ref=mine.at[pl.ds(pl.multiple_of(r * rows, 8), rows)], dst_ref=zparts.at[slot],
            send_sem=sems_c.at[0, r], recv_sem=sems_c.at[1, slot],
            device_id={"seq": r * 2 + core}, device_id_type=MESH,
        )

    def to_all(j, c, r):
        return pltpu.make_async_remote_copy(
            src_ref=zsum,
            dst_ref=out_ref.at[pl.ds(pl.multiple_of(c * HALF + r * rows, 8), rows)],
            send_sem=sems_d.at[0, j], recv_sem=sems_d.at[1, c * reducers + r],
            device_id={"seq": j}, device_id_type=MESH,
        )

    for o in range(chips):
        to_sib(lax.rem(dp + 1 + o, chips)).start()
    own = pl.ds(pl.multiple_of(core * HALF, 8), HALF)
    for o in range(chips):
        d = lax.rem(dp + 1 + o, chips)
        to_sib(d).wait_recv()
        part[pl.ds(d, 1)] = g_ref[pl.ds(d, 1), own] + pair[pl.ds(d, 1)]
        if o < chips - 1:
            to_chip(d, dp).start()
    total = part[dp]
    for o in range(1, chips):
        d = lax.rem(dp + chips - o, chips)
        to_chip(d, d).wait_recv()
        total = total + peers[d]
    mine[...] = total
    for r in range(reducers):
        @pl.when(r != z)
        def _():
            to_level(r, z).start()

    @pl.when(z < reducers)
    def _():
        acc = mine[pl.ds(pl.multiple_of(z * rows, 8), rows)]
        for o in range(1, depth):
            q = lax.rem(z + o, depth)
            to_level(z, q).wait_recv()
            acc = acc + zparts[q]
        zsum[...] = acc
        out_ref[pl.ds(pl.multiple_of(core * HALF + z * rows, 8), rows)] = acc
        for o in range(1, size):
            to_all(lax.rem(me + o, size), core, z).start()

    for c in range(2):
        for r in range(reducers):
            @pl.when(jnp.logical_or(c != core, r != z))
            def _():
                to_all(me, c, r).wait_recv()

    for o in range(chips):
        to_sib(lax.rem(dp + 1 + o, chips)).wait_send()
    for o in range(1, chips):
        to_chip(lax.rem(dp + o, chips), dp).wait_send()
    for r in range(reducers):
        @pl.when(r != z)
        def _():
            to_level(r, z).wait_send()

    @pl.when(z < reducers)
    def _():
        for o in range(1, size):
            to_all(lax.rem(me + o, size), core, z).wait_send()


def sds(shape, dtype=F32):
    return jax.ShapeDtypeStruct(shape, dtype)


def call_one(rec_lengths, fid_labels, u, gate, gg, x_proj, dt_proj, dt_bias, fid_bias, a2):
    return pl.pallas_call(
        phase_one,
        out_shape=(
            sds((KT, T, 128)), sds((KT, T, 128)), sds((KT, T, 128)),
            sds((L * N * S, 128)), sds((L * N * S, 128)), sds((KT, S, 128)),
            sds((KT, N * S, 128)), sds((KT, N * S, 128)), sds((KT, 40, 128)), sds((T, RANK), BF16),
        ),
        in_specs=[SMEM, SMEM] + [VMEM] * 8,
        out_specs=(VMEM,) * 10,
        scratch_shapes=[pltpu.VMEM((KT, N * S, 128), F32)],
        compiler_params=pltpu.CompilerParams(vmem_limit_bytes=40 << 20),
        name="phase_one",
    )(rec_lengths, fid_labels, u, gate, gg, x_proj, dt_proj, dt_bias, fid_bias, a2)


def call_exchange(send, a2):
    return pl.pallas_call(
        exchange,
        out_shape=sds((KT, 32, 128)),
        in_specs=[VMEM, VMEM],
        out_specs=VMEM,
        scratch_shapes=[
            pltpu.VMEM((16, 40, 128), F32), pltpu.VMEM((16, 32, 128), F32),
            pltpu.SemaphoreType.DMA((16,)), pltpu.SemaphoreType.DMA((16,)),
            pltpu.SemaphoreType.DMA((16,)), pltpu.SemaphoreType.DMA((16,)),
        ],
        compiler_params=pltpu.CompilerParams(collective_id=0, has_side_effects=True),
        name="exchange",
    )(send, a2)


def call_two(*operands):
    return pl.pallas_call(
        phase_two,
        out_shape=(
            sds((1, T, E), BF16), sds((1, T, E), BF16), sds((1, T, E), BF16), sds((KT, ROWS, 128)),
        ),
        in_specs=[SMEM, SMEM] + [VMEM] * 19,
        out_specs=(VMEM,) * 4,
        scratch_shapes=[
            pltpu.VMEM((KT, N * S, 128), F32), pltpu.VMEM((KT, N * S, 128), F32),
            pltpu.VMEM(((L + 1) * N * 2, S, 128), F32),
            pltpu.VMEM((L * N * S, 128), F32), pltpu.VMEM((L * N * S, 128), F32),
            pltpu.VMEM((KT, T, 128), F32), pltpu.VMEM((KT, T, 128), F32), pltpu.VMEM((KT, T, 128), F32),
            pltpu.VMEM((KT, N * S, 128), F32), pltpu.VMEM((T, E), BF16), pltpu.VMEM((1, T, 128), F32),
        ],
        compiler_params=pltpu.CompilerParams(vmem_limit_bytes=56 << 20),
        name="phase_two",
    )(*operands)


def call_reduce(grads):
    return pl.pallas_call(
        reduce_grads,
        out_shape=sds((ROWS, 128)),
        in_specs=[VMEM],
        out_specs=VMEM,
        scratch_shapes=[
            pltpu.VMEM((16, HALF, 128), F32), pltpu.VMEM((16, HALF, 128), F32),
            pltpu.VMEM((16, HALF, 128), F32), pltpu.VMEM((HALF, 128), F32),
            pltpu.VMEM((8, HALF // 6, 128), F32), pltpu.VMEM((HALF // 6, 128), F32),
            pltpu.SemaphoreType.DMA((2, 16)), pltpu.SemaphoreType.DMA((2, 16)),
            pltpu.SemaphoreType.DMA((2, 8)), pltpu.SemaphoreType.DMA((2, 16)),
        ],
        compiler_params=pltpu.CompilerParams(collective_id=1, has_side_effects=True),
        name="reduce_grads",
    )(grads)


def per_device(
    ssm_input, gate_input, grad_gated, x_proj, dt_proj, dt_bias, fid_bias, a_log, skip_gain,
    rec_lengths, fid_labels,
):
    a2 = (-LOG2E * jnp.exp(a_log)).T
    dtb = dt_bias[None, :]
    common = (
        rec_lengths, fid_labels, ssm_input, gate_input, grad_gated, x_proj, dt_proj, dtb, fid_bias, a2,
    )
    step, su, gy, bb, cb, segs, hs, acc, send, low = call_one(*common)
    starts = call_exchange(send, a2)
    gated, grad_input, grad_gate, grads = call_two(
        *common, skip_gain[None, :], step, su, gy, bb, cb, segs, hs, acc, starts, low
    )
    total = call_reduce(grads)
    base = COLS + RANK
    return (
        gated,
        grad_input,
        grad_gate,
        total[:COLS].T,
        total[COLS:base],
        total[base : base + N].T,
        total[base + N],
        total[base + N + 1],
        total[base + N + 2 : base + N + 4],
    )


def solution(mesh):
    wide = P("dp", "seq", None)
    in_specs = (wide, wide, wide, P(), P(), P(), P(), P(), P(), P("dp"), P("dp"))
    out_specs = (
        wide, wide, wide, P("dp", None), P(None, "dp"), P("dp", None), P("dp"), P("dp"), P(None, "dp"),
    )
    return jax.shard_map(
        per_device, mesh=mesh, in_specs=in_specs, out_specs=out_specs, check_vma=False
    )
```

time: 823 us -> 133 us (0.16); the launches traced: 812 us -> 132 us
  waiting for transfers between devices: 312 us -> 0 us
  local copies, waits for them, and re-layouts: 223 us -> 22.3 us
  other arithmetic: 155 us -> 0.93 us
  Pallas kernels: 0 us -> 107 us
  starting transfers between devices: 94.8 us -> 0 us
  between operations: 15.8 us -> 2.02 us
    ppermute x30 -> x0, waiting for transfers between devices: 114 us -> none  [passed_along(): return lax.ppermute(block, axis, route)]
    pallas_call x0 -> x4, Pallas kernels: none -> 107 us  [the longest x1 34.9 us: call_two(): pl.pallas_call(phase_two, out_shape=(sds((1, T, E), BF16), sds((1, T, E),...]
    psum x1 -> x0, waiting for transfers between devices: 104 us -> none  [per_device(): totals = lax.psum(packed, 'seq')]
    slice x69 -> x2, local copies, waits for them, and re-layouts: 105 us -> 2.61 us  [the longest x1 1.37 us: per_device(): total[COLS:base]]
    ppermute x30 -> x0, starting transfers between devices: 94.7 us -> none  [passed_along(): return lax.ppermute(block, axis, route)]
    reduce_scatter x1 -> x0, waiting for transfers between devices: 93.7 us -> none  [per_device(): shares = lax.psum_scatter(totals, 'dp', scatter_dimension=0, tiled=True)]
    reduce_sum x129 -> x0, other arithmetic: 76.2 us -> none  [the longest x80 36.7 us: run_block(): outputs.append(jnp.sum(c_blk[position][:, None] * h_now, axis=0))]
    dynamic_slice x64 -> x0, local copies, waits for them, and re-layouts: 44.5 us -> none  [forward_record(): h_last, (checks, outputs) = lax.scan(advance, h_start, blocks)]
  transfers between devices with their start and end apart: 32 -> 0, of which waited for: 32 -> 0; matrix products, arithmetic and copies ran while one was open for 0% -> 0% of each run, Pallas kernels for 0% -> 0%
where the time goes in v1:
time: 133 us; the launch traced here: 132 us
  Pallas kernels  107 us (80%)
  local copies, waits for them, and re-layouts  22.3 us (17%)
  between operations  2.02 us (2%)
    pallas_call x1, Pallas kernels, call_two(): pl.pallas_call(phase_two, out_shape=(sds((1, T, E), BF16), sds((1, T, E),...  34.9 us
    pallas_call x1, Pallas kernels, call_reduce(): pl.pallas_call(reduce_grads, out_shape=sds((ROWS, 128)), in_specs=[VMEM],...  32.5 us
    pallas_call x1, Pallas kernels, call_exchange(): pl.pallas_call(exchange, out_shape=sds((KT, 32, 128)), in_specs=[VMEM, VM...  28.7 us
    unnamed x37, local copies, waits for them, and re-layouts  15.7 us
    pallas_call x1, Pallas kernels, call_one(): pl.pallas_call(phase_one, out_shape=(sds((KT, T, 128)), sds((KT, T, 128))...  11.2 us

profile of v1, /device:TPU:1, one launch (start us, length us, event | category | flops | bytes accessed | tf_op | source)
XLA Modules:
  0.0 132.4 jit_solution(15168359100054769224)
XLA Ops:
  1.9 0.9 multiply_bitcast_fusion.a2_ref
  2.9 0.0 copy-start.1
  2.9 1.3 copy.21.xp_ref
  4.2 0.0 copy-start.2
  4.2 1.0 copy-done.2
  5.3 1.0 copy-done.3
  6.3 1.0 copy-done.4
  7.3 0.9 copy-done.12
  8.3 0.7 copy-done.15
  9.0 0.7 copy-done.17
  9.7 11.2 %phase_one.1 = (f32[16,128,128]{2,1,0:T(8,128)S(1)}, f32[16,128,128]{2,1,0:T(8,128)S(1)}, f32[16,128,128]{2,1,0:T(8,128)S(1)}, f32[2048,128]{1,0:T(8,128)S(1)}, ...) custom-call(s32[1]{0:T(128)S(6)} %copy.22.len_ref, ...), custom_call_target="tpu_custom_call" | custom-call | tf_op jit(solution)/shard_map/phase_one/pallas_call | solution.py:527
  20.9 0.0 copy-done.1
  20.9 0.0 copy-start.5
  20.9 1.0 copy-done.5
  21.9 1.0 copy-done.6
  22.8 1.0 copy-done.7
  23.8 1.0 copy-done.8
  24.8 1.0 copy-done.9
  25.8 1.0 copy-done.10
  26.8 1.0 copy-done.11
  27.8 0.7 copy-done.13
  28.5 0.6 copy-done.14
  29.2 0.6 copy-done.16
  29.8 28.7 %exchange.1.st_ref = f32[16,32,128]{2,1,0:T(8,128)} custom-call(f32[16,40,128]{2,1,0:T(8,128)} %copy-done.13, f32[16,2048]{1,0:T(8,128)} %copy-done.1), custom_call_target="tpu_custom_call" | custom-call | tf_op jit(solution)/shard_map/exchange/pallas_call | solution.py:543
  58.4 0.0 copy-done
  58.4 34.9 %phase_two.1 = (bf16[1,128,2048]{2,1,0:T(8,128)(2,1)}, bf16[1,128,2048]{2,1,0:T(8,128)(2,1)}, bf16[1,128,2048]{2,1,0:T(8,128)(2,1)}, f32[16,192,128]{2,1,0:T(8,128)}) custom-call(s32[1]{0:T(128)S(6)} %copy.22.len_ref, s32[1]{0:T(128)S(6)} %copy.23.lab_ref, bf16[1,128,2048]{2,1,0:T(8,128)(2,1)} %u_ref.3, bf16[1,128,2048]{2,1,0:T(8,128)(2,1)} %gate_ref.3, ...), custom_call_target="tpu_custom_call" | custom-call | tf_op jit(solution)/shard_map/phase_two/pallas_call | solution.py:559
  93.3 32.5 %reduce_grads.1 = f32[192,128]{1,0:T(8,128)} custom-call(f32[16,192,128]{2,1,0:T(8,128)} %get-tuple-element.36.g_ref), custom_call_target="tpu_custom_call" | custom-call | tf_op jit(solution)/shard_map/reduce_grads/pallas_call | solution.py:579
  125.8 1.2 slice.23
  127.0 1.3 slice_bitcast_fusion.2
  128.3 1.3 slice_bitcast_fusion.1
  129.6 1.4 %slice.19 = f32[64,128]{1,0:T(8,128)} slice(f32[192,128]{1,0:T(8,128)} %reduce_grads.1), slice={[96:160], [0:128]} | slice | bytes 65536 | tf_op jit(solution)/shard_map/slice | solution.py:617
  131.0 1.4 %slice_bitcast_fusion = f32[128,96]{0,1:T(8,128)} fusion(f32[192,128]{1,0:T(8,128)} %reduce_grads.1), kind=kLoop, calls=%fused_computation.1 | loop fusion | bytes 98304 | tf_op jit(solution)/shard_map/transpose | solution.py:616
  (15 shorter events, 0.0 us)
Async XLA Ops:
  2.9 18.0 %copy-start.1 = (f32[16,2048]{1,0:T(8,128)}, f32[16,2048]{1,0:T(8,128)S(1)}, u32[]{:S(2)}) copy-start(f32[16,2048]{1,0:T(8,128)S(1)} %multiply_bitcast_fusion.a2_ref) | copy-start | bytes 393220
  4.2 1.0 copy-start.2
  5.2 1.0 copy-start.3
  6.3 1.0 copy-start.4
  7.3 0.9 copy-start.12
  8.3 0.7 copy-start.15
  9.0 0.7 copy-start.17
  9.7 48.7 %copy-start = (bf16[2048,96]{1,0:T(8,128)(2,1)}, bf16[2048,96]{1,0:T(8,128)(2,1)S(1)}, u32[]{:S(2)}) copy-start(bf16[2048,96]{1,0:T(8,128)(2,1)S(1)} %copy.21.xp_ref) | copy-start | bytes 1179652
  20.9 1.0 copy-start.5
  21.9 1.0 copy-start.6
  22.8 1.0 copy-start.7
  23.8 1.0 copy-start.8
  24.8 1.0 copy-start.9
  25.8 1.0 copy-start.10
  26.8 1.0 copy-start.11
  27.8 0.7 copy-start.13
  28.5 0.6 copy-start.14
  29.2 0.6 copy-start.16

commit v2 on v1

v2 whole, which is shorter than its diff:
```python
import jax
import jax.numpy as jnp
from jax import lax
from jax.experimental import pallas as pl
from jax.experimental.pallas import tpu as pltpu
from jax.sharding import PartitionSpec as P

F32 = jnp.float32
BF16 = jnp.bfloat16
LOG2E = 1.4426950408889634
LN2 = 0.6931471805599453
T = 128
E = 2048
N = 16
RANK = 64
KT = E // 128
S = 8
L = T // S
COLS = RANK + 2 * N
ROWS = 96
HALF = ROWS // 2
MESH = pl.DeviceIdType.MESH
VMEM = pl.BlockSpec(memory_space=pltpu.VMEM)
ANY = pl.BlockSpec(memory_space=pl.ANY)
SMEM = pl.BlockSpec(memory_space=pltpu.SMEM)


def lanes(k):
    return pl.ds(pl.multiple_of(k * 128, 128), 128)


def store_permuted(ref, k, value):
    for blk in range(T // 8):
        first = (blk % 2) * 64 + blk // 2
        ref[k, pl.ds(first, 8, stride=8), :] = value[blk * 8 : blk * 8 + 8, :]


def load_natural(ref, k):
    parts = []
    for blk in range(T // 8):
        first = (blk % 2) * 64 + blk // 2
        parts.append(ref[k, pl.ds(first, 8, stride=8), :])
    return jnp.concatenate(parts, axis=0)


def sigmoid(v):
    return 1.0 / (1.0 + jnp.exp(-v))


def softplus(v):
    z = jnp.exp(-jnp.abs(v))
    r = z / (z + 2.0)
    q = r * r
    poly = 1.0 / 15.0
    for odd in (13.0, 11.0, 9.0, 7.0, 5.0, 3.0, 1.0):
        poly = poly * q + 1.0 / odd
    return jnp.maximum(v, 0.0) + 2.0 * r * poly


def live_mask(len_ref):
    t0 = lax.axis_index("seq") * T
    pos = t0 + lax.broadcasted_iota(jnp.int32, (T, 128), 0)
    return (pos < len_ref[0]).astype(F32)


def fid_row(lab_ref, fid_ref, ls):
    label = lab_ref[0]
    row = jnp.zeros((1, 128), F32)
    for kind in range(2):
        row = row + jnp.where(label == kind, fid_ref[kind : kind + 1, ls], 0.0)
    return row


def row8(ref, n, ls):
    return jnp.broadcast_to(ref[n : n + 1, ls], (8, 128))


def tile8(n):
    return pl.ds(pl.multiple_of(n * S, S), S)


def step_kernel(
    len_ref, lab_ref, u_hbm, gate_hbm, gg_hbm, xp_hbm, dtp_hbm, dtb_hbm, fid_hbm, al_hbm, skip_hbm,
    gated_hbm, gin_hbm, ggate_hbm, tot_ref,
    u_ref, gate_ref, gg_ref, xp_ref, dtp_ref, dtb_ref, fid_ref, al_ref, skip_ref, a2_ref, a2w,
    low_ref, step_ref, su_ref, gy_ref, bb_ref, cb_ref, segs_ref, hs_ref, as_ref,
    send_h, send_a, got_h, got_a, back_h, back_a, st_h, st_a,
    hbuf, bgr, cgr, ybuf, sbuf, gbuf, agbuf, dtg, dirs, sl_ref, zg_ref, ds_ref,
    gated_ref, gin_ref, ggate_ref, grads, pair, part, peers, mine, zparts,
    in_sems, out_sems, x_send, x_recv, pair_send, pair_recv, chip_send, chip_recv,
    z_send, z_recv, fin_send, fin_recv,
):
    chips = lax.axis_size("dp")
    size = lax.axis_size("seq")
    depth = size // 2
    dp = lax.axis_index("dp")
    me = lax.axis_index("seq")
    z = me // 2
    core = lax.rem(me, 2)
    sib = me + 1 - 2 * core

    loads = []
    pairs = (
        (u_hbm.at[0], u_ref), (xp_hbm, xp_ref), (dtp_hbm, dtp_ref), (dtb_hbm, dtb_ref), (fid_hbm, fid_ref),
        (gate_hbm.at[0], gate_ref), (gg_hbm.at[0], gg_ref), (al_hbm, al_ref), (skip_hbm, skip_ref),
    )
    for i, (src, dst) in enumerate(pairs):
        copy = pltpu.make_async_copy(src, dst, in_sems.at[i])
        copy.start()
        loads.append(copy)

    barrier = pltpu.get_barrier_semaphore()
    for o in range(1, chips):
        d = lax.rem(dp + o, chips)
        pl.semaphore_signal(barrier, inc=1, device_id={"dp": d}, device_id_type=MESH)
    for o in range(1, size):
        j = lax.rem(me + o, size)
        pl.semaphore_signal(barrier, inc=1, device_id={"seq": j}, device_id_type=MESH)

    def remote(src, dst, send, recv, where):
        return pltpu.make_async_remote_copy(
            src_ref=src, dst_ref=dst, send_sem=send, recv_sem=recv, device_id=where, device_id_type=MESH
        )

    def hop(which, src, dst, j, slot):
        return remote(src.at[j], dst.at[slot], x_send.at[which, j], x_recv.at[which, slot], {"seq": j})

    def there_h(j, slot):
        return hop(0, send_h, got_h, j, slot)

    def there_a(j, slot):
        return hop(1, send_a, got_a, j, slot)

    def home_h(j, slot):
        return hop(2, back_h, st_h, j, slot)

    def home_a(j, slot):
        return hop(3, back_a, st_a, j, slot)

    def to_sib(p, d):
        return remote(
            grads.at[p, d, pl.ds(pl.multiple_of((1 - core) * HALF, 8), HALF)], pair.at[p, d],
            pair_send.at[p, d], pair_recv.at[p, d], {"seq": sib},
        )

    def to_chip(p, d, slot):
        return remote(
            part.at[p, d], peers.at[p, slot], chip_send.at[p, d], chip_recv.at[p, slot], {"dp": d}
        )

    def to_level(p, q, slot):
        return remote(
            mine.at[p], zparts.at[p, slot], z_send.at[p, q], z_recv.at[p, slot], {"seq": q * 2 + core}
        )

    def to_final(p):
        return remote(
            tot_ref.at[p, pl.ds(pl.multiple_of(core * HALF, 8), HALF)],
            tot_ref.at[p, pl.ds(pl.multiple_of(core * HALF, 8), HALF)],
            fin_send.at[p], fin_recv.at[p], {"seq": sib},
        )

    def from_final(p):
        return remote(
            tot_ref.at[p, pl.ds(pl.multiple_of((1 - core) * HALF, 8), HALF)],
            tot_ref.at[p, pl.ds(pl.multiple_of((1 - core) * HALF, 8), HALF)],
            fin_send.at[p], fin_recv.at[p], {"seq": sib},
        )

    loads[0].wait()
    loads[1].wait()
    proj = lax.dot_general(
        u_ref[...], xp_ref[...], (((1,), (1,)), ((), ())), preferred_element_type=F32
    )
    low_ref[...] = proj[:, :RANK].astype(BF16)
    for n in range(N):
        for col, ref in ((RANK + n, bb_ref), (RANK + N + n, cb_ref)):
            wide = jnp.broadcast_to(proj[:, col : col + 1], (T, 128))
            for blk in range(T // 8):
                first = (blk % 2) * 8 * (N * S) + n * S + blk // 2
                ref[pl.ds(first, 8, stride=N * S), :] = wide[blk * 8 : blk * 8 + 8, :]
    for copy in loads[2:]:
        copy.wait()
    a2_ref[...] = -LOG2E * jnp.exp(al_ref[...])
    live = live_mask(len_ref)

    @pl.loop(0, KT)
    def _(k):
        ls = lanes(k)
        dt_raw = (
            jnp.dot(low_ref[...], dtp_ref[:, ls], preferred_element_type=F32)
            + dtb_ref[:, ls]
            + fid_row(lab_ref, fid_ref, ls)
        )
        step = softplus(dt_raw) * live
        u = u_ref[:, ls].astype(F32)
        store_permuted(step_ref, k, step)
        store_permuted(su_ref, k, step * u)
        for n in range(N):
            a2w[k, n * S : n * S + S, :] = row8(a2_ref, n, ls)

    GK = 2

    @pl.loop(0, KT // GK)
    def _(kp):
        ks = [kp * GK + i for i in range(GK)]
        GN = 8

        @pl.loop(0, N // GN)
        def _(ng):
            ns = [ng * GN + j for j in range(GN)]
            a2 = [[a2w[k, tile8(n), :] for k in ks] for n in ns]

            def ahead(tau, hh):
                rows = tile8(tau)
                st = [step_ref[k, rows, :] for k in ks]
                su = [su_ref[k, rows, :] for k in ks]
                out = []
                for j, n in enumerate(ns):
                    b = bb_ref[tile8(tau * N + n), :]
                    for i in range(GK):
                        out.append(jnp.exp2(a2[j][i] * st[i]) * hh[j * GK + i] + b * su[i])
                return tuple(out)

            zero = jnp.zeros((S, 128), F32)
            ends = lax.fori_loop(0, L, ahead, (zero,) * (GN * GK), unroll=16)
            for j, n in enumerate(ns):
                for i, k in enumerate(ks):
                    hs_ref[k, tile8(n), :] = ends[j * GK + i]

    @pl.loop(0, KT)
    def _(k):
        seg = step_ref[k, pl.ds(0, S), :]
        for tau in range(1, L):
            seg = seg + step_ref[k, pl.ds(tau * S, S), :]
        segs_ref[k] = seg
        for nh in range(2):
            a2 = a2_ref[nh * 8 : nh * 8 + 8, lanes(k)]
            h = hs_ref[k, pl.ds(nh * 64, 8, stride=8), :]
            for s in range(1, S):
                h = jnp.exp2(a2 * seg[s : s + 1, :]) * h + hs_ref[k, pl.ds(nh * 64 + s, 8, stride=8), :]
            send_h[k, pl.ds(nh * 8, 8), :] = h
        total = jnp.sum(seg, axis=0, keepdims=True)
        send_h[k, pl.ds(16, 8), :] = jnp.broadcast_to(total, (8, 128))

    pl.semaphore_wait(barrier, chips + size - 2)
    for o in range(1, size):
        there_h(lax.rem(me + o, size), me).start()
    got_h[pl.ds(me, 1)] = send_h[pl.ds(me, 1)]

    @pl.loop(0, KT)
    def _(k):
        ls = lanes(k)
        gate = gate_ref[:, ls].astype(F32)
        sig = sigmoid(gate)
        silu = gate * sig * live
        gg = gg_ref[:, ls].astype(F32)
        sl_ref[:, ls] = silu
        zg_ref[:, ls] = gg * live * (sig * (1.0 + gate * (1.0 - sig)))
        store_permuted(gy_ref, k, gg * silu)

    @pl.loop(0, KT // GK)
    def _(kp):
        ks = [kp * GK + i for i in range(GK)]
        GN = 4

        @pl.loop(0, N // GN)
        def _(ng):
            ns = [ng * GN + j for j in range(GN)]
            a2 = [[a2w[k, tile8(n), :] for k in ks] for n in ns]

            def pull(tau, state):
                rows = tile8(tau)
                cum = [state[i] + step_ref[k, rows, :] for i, k in enumerate(ks)]
                gy = [gy_ref[k, rows, :] for k in ks]
                out = list(cum)
                for j, n in enumerate(ns):
                    c = cb_ref[tile8(tau * N + n), :]
                    for i in range(GK):
                        acc = state[GK + j * GK + i]
                        out.append(acc + jnp.exp2(a2[j][i] * cum[i]) * (c * gy[i]))
                return tuple(out)

            zero = jnp.zeros((S, 128), F32)
            ends = lax.fori_loop(0, L, pull, (zero,) * (GK + GN * GK), unroll=16)
            for j, n in enumerate(ns):
                for i, k in enumerate(ks):
                    as_ref[k, tile8(n), :] = ends[GK + j * GK + i]

    @pl.loop(0, KT)
    def _(k):
        for nh in range(2):
            a2 = a2_ref[nh * 8 : nh * 8 + 8, lanes(k)]
            g = as_ref[k, pl.ds(nh * 64 + S - 1, 8, stride=8), :]
            for s in range(S - 2, -1, -1):
                p = jnp.exp2(a2 * segs_ref[k, s : s + 1, :])
                g = p * g + as_ref[k, pl.ds(nh * 64 + s, 8, stride=8), :]
            send_a[k, pl.ds(nh * 8, 8), :] = g

    for o in range(1, size):
        there_a(lax.rem(me + o, size), me).start()
    got_a[pl.ds(me, 1)] = send_a[pl.ds(me, 1)]

    bgr[...] = jnp.zeros_like(bgr)
    cgr[...] = jnp.zeros_like(cgr)

    a2_mine = a2_ref[:, lanes(me)]
    for o in range(1, size):
        j = lax.rem(me + o, size)
        there_h(j, j).wait_recv()
    h = jnp.zeros((N, 128), F32)
    for i in range(size):
        back_h[i] = h
        h = jnp.exp2(a2_mine * got_h[i, 16:17, :]) * h + got_h[i, 0:16, :]
    for o in range(1, size):
        home_h(lax.rem(me + o, size), me).start()
    st_h[pl.ds(me, 1)] = back_h[pl.ds(me, 1)]

    @pl.loop(0, KT)
    def _(k):
        ls = lanes(k)
        dt_raw = (
            jnp.dot(low_ref[...], dtp_ref[:, ls], preferred_element_type=F32)
            + dtb_ref[:, ls]
            + fid_row(lab_ref, fid_ref, ls)
        )
        ds_ref[:, ls] = live * sigmoid(dt_raw)

    for o in range(1, size):
        j = lax.rem(me + o, size)
        there_a(j, j).wait_recv()
    g = jnp.zeros((N, 128), F32)
    for i in range(size - 1, -1, -1):
        back_a[i] = g
        g = jnp.exp2(a2_mine * got_h[i, 16:17, :]) * g + got_a[i]
    for o in range(1, size):
        home_a(lax.rem(me + o, size), me).start()
    st_a[pl.ds(me, 1)] = back_a[pl.ds(me, 1)]

    for o in range(1, size):
        j = lax.rem(me + o, size)
        home_h(j, j).wait_recv()

    @pl.loop(0, KT)
    def _(k):
        for nh in range(2):
            a2 = a2_ref[nh * 8 : nh * 8 + 8, lanes(k)]
            h = st_h[k, nh * 8 : nh * 8 + 8, :]
            for s in range(S):
                at = pl.ds(nh * 64 + s, 8, stride=8)
                end = hs_ref[k, at, :]
                hs_ref[k, at, :] = h
                if s + 1 < S:
                    h = jnp.exp2(a2 * segs_ref[k, s : s + 1, :]) * h + end

    @pl.loop(0, KT // GK)
    def _(kp):
        ks = [kp * GK + i for i in range(GK)]
        FN = 8
        for ng in range(N // FN):
            ns = [ng * FN + j for j in range(FN)]
            a2 = [[a2w[k, n * S : n * S + S, :] for k in ks] for n in ns]
            first = []
            for n in ns:
                for i, k in enumerate(ks):
                    h = hs_ref[k, n * S : n * S + S, :]
                    hbuf[kp * (L + 1) * N * GK + n * GK + i] = h
                    first.append(h)

            def forward(tau, hh):
                rows = tile8(tau)
                st = [step_ref[k, rows, :] for k in ks]
                su = [su_ref[k, rows, :] for k in ks]
                gy = [gy_ref[k, rows, :] for k in ks]
                ys = [None] * GK
                out = []
                for j, n in enumerate(ns):
                    at = tile8(tau * N + n)
                    b = bb_ref[at, :]
                    c = cb_ref[at, :]
                    cg = None
                    for i in range(GK):
                        h = jnp.exp2(a2[j][i] * st[i]) * hh[j * GK + i] + b * su[i]
                        out.append(h)
                        hbuf[(kp * (L + 1) + tau + 1) * (N * GK) + n * GK + i] = h
                        term = c * h
                        ys[i] = term if ys[i] is None else ys[i] + term
                        term = h * gy[i]
                        cg = term if cg is None else cg + term
                    cgr[at, :] = cgr[at, :] + cg
                for i, k in enumerate(ks):
                    if ng == 0:
                        ybuf[k, rows, :] = ys[i]
                    else:
                        ybuf[k, rows, :] = ybuf[k, rows, :] + ys[i]
                return tuple(out)

            lax.fori_loop(0, L, forward, tuple(first), unroll=16)

    for o in range(1, size):
        j = lax.rem(me + o, size)
        home_a(j, j).wait_recv()

    @pl.loop(0, KT)
    def _(k):
        for nh in range(2):
            a2 = a2_ref[nh * 8 : nh * 8 + 8, lanes(k)]
            g = st_a[k, nh * 8 : nh * 8 + 8, :]
            for s in range(S - 1, -1, -1):
                at = pl.ds(nh * 64 + s, 8, stride=8)
                end = as_ref[k, at, :]
                as_ref[k, at, :] = g
                if s > 0:
                    g = jnp.exp2(a2 * segs_ref[k, s : s + 1, :]) * g + end

    @pl.loop(0, KT // GK)
    def _(kp):
        ks = [kp * GK + i for i in range(GK)]
        BN = 4
        for ng in range(N // BN):
            ns = [ng * BN + j for j in range(BN)]
            a2 = [[a2w[k, n * S : n * S + S, :] for k in ks] for n in ns]
            carry = [as_ref[k, n * S : n * S + S, :] for n in ns for k in ks]
            zero = jnp.zeros((S, 128), F32)

            def behind(turn, state):
                tau = L - 1 - turn
                cs, ags = state
                rows = tile8(tau)
                st = [step_ref[k, rows, :] for k in ks]
                su = [su_ref[k, rows, :] for k in ks]
                gy = [gy_ref[k, rows, :] for k in ks]
                sb = [None] * GK
                sg = [None] * GK
                new_c, new_a = [], []
                for j, n in enumerate(ns):
                    at = tile8(tau * N + n)
                    b = bb_ref[at, :]
                    c = cb_ref[at, :]
                    bg = None
                    for i in range(GK):
                        g = c * gy[i] + cs[j * GK + i]
                        term = g * b
                        sb[i] = term if sb[i] is None else sb[i] + term
                        term = g * su[i]
                        bg = term if bg is None else bg + term
                        dg = jnp.exp2(a2[j][i] * st[i]) * g
                        w = dg * hbuf[(kp * (L + 1) + tau) * (N * GK) + n * GK + i]
                        term = a2[j][i] * w
                        sg[i] = term if sg[i] is None else sg[i] + term
                        new_c.append(dg)
                        new_a.append(ags[j * GK + i] + st[i] * w)
                    bgr[at, :] = bgr[at, :] + bg
                for i, k in enumerate(ks):
                    if ng == 0:
                        sbuf[k, rows, :] = sb[i]
                        gbuf[k, rows, :] = sg[i]
                    else:
                        sbuf[k, rows, :] = sbuf[k, rows, :] + sb[i]
                        gbuf[k, rows, :] = gbuf[k, rows, :] + sg[i]
                return tuple(new_c), tuple(new_a)

            _, ags = lax.fori_loop(0, L, behind, (tuple(carry), (zero,) * (BN * GK)), unroll=16)
            for j, n in enumerate(ns):
                for i, k in enumerate(ks):
                    agbuf[k, n * S : n * S + S, :] = ags[j * GK + i]

    label = lab_ref[0]
    own = pl.ds(pl.multiple_of(core * HALF, 8), HALF)

    def pass_on(p, i):
        d = lax.rem(dp + 1 + i, chips)
        to_sib(p, d).wait_recv()
        part[p, pl.ds(d, 1)] = grads[p, pl.ds(d, 1), own] + pair[p, pl.ds(d, 1)]

    @pl.loop(0, KT)
    def _(i):
        k = lax.rem(dp + 1 + i, chips)
        ls = lanes(k)
        u = u_ref[:, ls].astype(F32)
        silu = sl_ref[:, ls]
        y = load_natural(ybuf, k) + skip_ref[:, ls] * u
        gated_ref[:, ls] = (y * silu).astype(BF16)
        ggate_ref[:, ls] = (y * zg_ref[:, ls]).astype(BF16)
        step_grad = LN2 * load_natural(gbuf, k) + u * load_natural(sbuf, k)
        dt_grad = step_grad * ds_ref[:, ls]
        dt_b = dt_grad.astype(BF16)
        dtg[:, ls] = dt_b
        grads[0, k, 0:RANK, :] = lax.dot_general(
            low_ref[...], dt_b, (((0,), (0,)), ((), ())), preferred_element_type=F32
        )
        for nh in range(2):
            ag = agbuf[k, pl.ds(nh * 64, 8, stride=8), :]
            for s in range(1, S):
                ag = ag + agbuf[k, pl.ds(nh * 64 + s, 8, stride=8), :]
            grads[0, k, RANK + nh * 8 : RANK + nh * 8 + 8, :] = (
                ag * a2_ref[nh * 8 : nh * 8 + 8, ls] * LN2
            )
        skip_row = jnp.sum(gg_ref[:, ls].astype(F32) * silu * u, axis=0, keepdims=True)
        dt_row = jnp.sum(dt_grad, axis=0, keepdims=True)
        zero = jnp.zeros_like(dt_row)
        grads[0, k, RANK + N : RANK + N + 8, :] = jnp.concatenate(
            [
                skip_row,
                dt_row,
                jnp.where(label == 0, dt_row, zero),
                jnp.where(label == 1, dt_row, zero),
                zero, zero, zero, zero,
            ],
            axis=0,
        )
        grads[0, k, RANK + N + 8 : ROWS, :] = jnp.zeros((ROWS - RANK - N - 8, 128), F32)
        to_sib(0, k).start()

        @pl.when(i > 0)
        def _():
            pass_on(0, i - 1)
            d = lax.rem(dp + i, chips)
            to_chip(0, d, dp).start()

    pass_on(0, KT - 1)
    out_gated = pltpu.make_async_copy(gated_ref, gated_hbm.at[0], out_sems.at[0])
    out_gated.start()
    out_ggate = pltpu.make_async_copy(ggate_ref, ggate_hbm.at[0], out_sems.at[1])
    out_ggate.start()

    low_grad = lax.dot_general(
        dtg[...], dtp_ref[...], (((1,), (1,)), ((), ())), preferred_element_type=F32
    )
    lane = lax.broadcasted_iota(jnp.int32, (128, 128), 1)
    sums = jnp.zeros((T, 128), F32)
    for n in range(N):
        for col, ref in ((RANK + n, bgr), (RANK + N + n, cgr)):
            tile = jnp.concatenate(
                [ref[(tau * N + n) * S : (tau * N + n) * S + S, :] for tau in range(L)], axis=0
            )
            hi = tile.astype(BF16)
            lo = (tile - hi.astype(F32)).astype(BF16)
            pick = (lane == col).astype(BF16)
            sums = sums + jnp.dot(hi, pick, preferred_element_type=F32)
            sums = sums + jnp.dot(lo, pick, preferred_element_type=F32)
    dirs[0] = sums
    sums = load_natural(dirs, 0)
    proj_grad = jnp.concatenate([low_grad, sums[:, RANK:COLS]], axis=1).astype(BF16)

    @pl.loop(0, KT)
    def _(i):
        k = lax.rem(dp + 1 + i, chips)
        grads[1, k] = lax.dot_general(
            proj_grad, u_ref[:, lanes(k)], (((0,), (0,)), ((), ())), preferred_element_type=F32
        )
        to_sib(1, k).start()

        @pl.when(i > 0)
        def _():
            pass_on(1, i - 1)
            d = lax.rem(dp + i, chips)
            to_chip(1, d, dp).start()

    pass_on(1, KT - 1)

    @pl.loop(0, KT)
    def _(k):
        ls = lanes(k)
        back = jnp.dot(proj_grad, xp_ref[:, ls], preferred_element_type=F32)
        direct = load_natural(step_ref, k) * load_natural(sbuf, k)
        straight = gg_ref[:, ls].astype(F32) * sl_ref[:, ls] * skip_ref[:, ls]
        gin_ref[:, ls] = (direct + straight + back).astype(BF16)

    out_gin = pltpu.make_async_copy(gin_ref, gin_hbm.at[0], out_sems.at[2])
    out_gin.start()

    for p in range(2):
        total = part[p, dp]
        for o in range(1, chips):
            d = lax.rem(dp + chips - o, chips)
            to_chip(p, d, d).wait_recv()
            total = total + peers[p, d]
        mine[p] = total
        for o in range(1, depth):
            to_level(p, lax.rem(z + o, depth), z).start()
    for p in range(2):
        total = mine[p]
        for o in range(1, depth):
            q = lax.rem(z + o, depth)
            to_level(p, q, q).wait_recv()
            total = total + zparts[p, q]
        tot_ref[p, own, :] = total
        to_final(p).start()
    for p in range(2):
        from_final(p).wait_recv()

    for o in range(1, size):
        j = lax.rem(me + o, size)
        there_h(j, me).wait_send()
        there_a(j, me).wait_send()
        home_h(j, me).wait_send()
        home_a(j, me).wait_send()
    for p in range(2):
        to_final(p).wait_send()
        for d in range(chips):
            to_sib(p, d).wait_send()
        for o in range(1, chips):
            to_chip(p, lax.rem(dp + o, chips), dp).wait_send()
        for o in range(1, depth):
            to_level(p, lax.rem(z + o, depth), z).wait_send()
    out_gated.wait()
    out_ggate.wait()
    out_gin.wait()


def finish(
    gated_in, gin_in, ggate_in, tot_ref,
    gated_out, gin_out, ggate_out, gx_ref, gdt_ref, ga_ref, gs_ref, gb_ref, gf_ref,
    hold, in_sems, out_sems,
):
    chunks = 2
    rows = T // chunks
    ins, outs = [], []
    for i, (src, dst) in enumerate(
        ((gated_in, gated_out), (gin_in, gin_out), (ggate_in, ggate_out))
    ):
        for q in range(chunks):
            at = pl.ds(q * rows, rows)
            one = i * chunks + q
            ins.append(pltpu.make_async_copy(src.at[0, at], hold.at[i, at], in_sems.at[one]))
            outs.append(pltpu.make_async_copy(hold.at[i, at], dst.at[0, at], out_sems.at[one]))
    for copy in ins:
        copy.start()
    base = RANK + N
    gx_ref[...] = tot_ref[1]
    gdt_ref[...] = tot_ref[0, 0:RANK, :]
    ga_ref[...] = tot_ref[0, RANK:base, :]
    gs_ref[...] = tot_ref[0, base : base + 1, :]
    gb_ref[...] = tot_ref[0, base + 1 : base + 2, :]
    gf_ref[...] = tot_ref[0, base + 2 : base + 4, :]
    for into, out in zip(ins, outs):
        into.wait()
        out.start()
    for out in outs:
        out.wait()


def sds(shape, dtype=F32):
    return jax.ShapeDtypeStruct(shape, dtype)


def vm(shape, dtype=F32):
    return pltpu.VMEM(shape, dtype)


def call_step(*operands):
    dma = pltpu.SemaphoreType.DMA
    big = sds((1, T, E), BF16)
    return pl.pallas_call(
        step_kernel,
        out_shape=(big, big, big, sds((2, ROWS, 128))),
        in_specs=[SMEM, SMEM] + [ANY] * 9,
        out_specs=(ANY, ANY, ANY, VMEM),
        scratch_shapes=[
            vm((T, E), BF16), vm((T, E), BF16), vm((T, E), BF16), vm((COLS, E), BF16), vm((RANK, E), BF16),
            vm((1, E)), vm((2, E)), vm((N, E)), vm((1, E)), vm((N, E)), vm((KT, N * S, 128)),
            vm((T, RANK), BF16), vm((KT, T, 128)), vm((KT, T, 128)), vm((KT, T, 128)),
            vm((L * N * S, 128)), vm((L * N * S, 128)), vm((KT, S, 128)),
            vm((KT, N * S, 128)), vm((KT, N * S, 128)),
            vm((16, 24, 128)), vm((16, 16, 128)), vm((16, 24, 128)), vm((16, 16, 128)),
            vm((16, 16, 128)), vm((16, 16, 128)), vm((16, 16, 128)), vm((16, 16, 128)),
            vm((KT * (L + 1) * N, S, 128)), vm((L * N * S, 128)), vm((L * N * S, 128)),
            vm((KT, T, 128)), vm((KT, T, 128)), vm((KT, T, 128)), vm((KT, N * S, 128)),
            vm((T, E), BF16), vm((1, T, 128)), vm((T, E)), vm((T, E)), vm((T, E)),
            vm((T, E), BF16), vm((T, E), BF16), vm((T, E), BF16),
            vm((2, 16, ROWS, 128)), vm((2, 16, HALF, 128)), vm((2, 16, HALF, 128)),
            vm((2, 16, HALF, 128)), vm((2, HALF, 128)), vm((2, 8, HALF, 128)),
            dma((9,)), dma((3,)), dma((4, 16)), dma((4, 16)), dma((2, 16)), dma((2, 16)),
            dma((2, 16)), dma((2, 16)), dma((2, 8)), dma((2, 8)), dma((2,)), dma((2,)),
        ],
        compiler_params=pltpu.CompilerParams(
            collective_id=0, has_side_effects=True, vmem_limit_bytes=60 << 20
        ),
        name="step_kernel",
    )(*operands)


def call_finish(*operands):
    big = sds((1, T, E), BF16)
    return pl.pallas_call(
        finish,
        out_shape=(
            big, big, big, sds((COLS, 128)), sds((RANK, 128)), sds((N, 128)), sds((1, 128)),
            sds((1, 128)), sds((2, 128)),
        ),
        in_specs=[ANY, ANY, ANY, VMEM],
        out_specs=(ANY, ANY, ANY) + (VMEM,) * 6,
        scratch_shapes=[
            vm((3, T, E), BF16), pltpu.SemaphoreType.DMA((6,)), pltpu.SemaphoreType.DMA((6,)),
        ],
        name="finish",
    )(*operands)


def per_device(
    ssm_input, gate_input, grad_gated, x_proj, dt_proj, dt_bias, fid_bias, a_log, skip_gain,
    rec_lengths, fid_labels,
):
    results = call_step(
        rec_lengths, fid_labels, ssm_input, gate_input, grad_gated, x_proj.T, dt_proj,
        dt_bias[None, :], fid_bias, a_log.T, skip_gain[None, :],
    )
    gated, gin, ggate, gx, gdt, ga, gs, gb, gf = call_finish(*results)
    return (gated, gin, ggate, gx.T, gdt, ga.T, gs[0], gb[0], gf)


def solution(mesh):
    wide = P("dp", "seq", None)
    in_specs = (wide, wide, wide, P(), P(), P(), P(), P(), P(), P("dp"), P("dp"))
    out_specs = (
        wide, wide, wide, P("dp", None), P(None, "dp"), P("dp", None), P("dp"), P("dp"), P(None, "dp"),
    )
    return jax.shard_map(
        per_device, mesh=mesh, in_specs=in_specs, out_specs=out_specs, check_vma=False
    )
```

time: 133 us -> 86.7 us (0.65)
  Pallas kernels: 107 us -> 84.6 us
  local copies, waits for them, and re-layouts: 22.3 us -> 0 us
    pallas_call x4 -> x2, Pallas kernels: 107 us -> 84.6 us  [the longest x1 80.8 us: call_step(): pl.pallas_call(step_kernel, out_shape=(big, big, big, sds((2, ROWS, 128))...]
    unnamed x37 -> x0, local copies, waits for them, and re-layouts: 15.7 us -> none
    transpose x2 -> x0, local copies, waits for them, and re-layouts: 2.72 us -> none  [the longest x1 1.42 us: per_device(): total[:COLS]]
    slice x2 -> x0, local copies, waits for them, and re-layouts: 2.61 us -> none  [the longest x1 1.37 us: per_device(): total[COLS:base]]
where the time goes in v2:
time: 86.7 us; the launch traced here: 86.5 us
  Pallas kernels  84.6 us (98%)
  between operations  1.95 us (2%)
    pallas_call x1, Pallas kernels, call_step(): pl.pallas_call(step_kernel, out_shape=(big, big, big, sds((2, ROWS, 128))...  80.8 us
    pallas_call x1, Pallas kernels, call_finish(): pl.pallas_call(finish, out_shape=(big, big, big, sds((COLS, 128)), sds((R...  3.72 us

profile of v2, /device:TPU:1, one launch (start us, length us, event | category | flops | bytes accessed | tf_op | source)
XLA Modules:
  0.0 86.5 jit_solution(17866453339810745529)
XLA Ops:
  1.9 80.8 %step_kernel.1 = (bf16[1,128,2048]{2,1,0:T(8,128)(2,1)}, bf16[1,128,2048]{2,1,0:T(8,128)(2,1)}, bf16[1,128,2048]{2,1,0:T(8,128)(2,1)}, f32[2,96,128]{2,1,0:T(8,128)}) custom-call(s32[1]{0:T(128)S(6)} %copy.20.len_ref, s32[1]{0:T(128)S(6)} %copy.21.lab_ref, bf16[1,128,2048]{2,1,0:T(8,128)(2,1)} %u_hbm.1, bf16[1,128,2048]{2,1,0:T(8,128)(2,1)} %gate_hbm.1, ...), custom_call_target="tpu_custom_call" | custom-call | tf_op jit(solution)/shard_map/step_kernel/pallas_call | solution.py:655
  82.8 3.7 %finish.1 = (bf16[1,128,2048]{2,1,0:T(8,128)(2,1)}, bf16[1,128,2048]{2,1,0:T(8,128)(2,1)}, bf16[1,128,2048]{2,1,0:T(8,128)(2,1)}, f32[96,128]{1,0:T(8,128)}, f32...) custom-call(bf16[1,128,2048]{2,1,0:T(8,128)(2,1)} %get-tuple-element.22.gated, ...), custom_call_target="tpu_custom_call" | custom-call | tf_op jit(solution)/shard_map/finish/pallas_call | solution.py:686

commit v3 on v2

v3 whole, which is shorter than its diff:
```python
import jax
import jax.numpy as jnp
from jax import lax
from jax.experimental import pallas as pl
from jax.experimental.pallas import tpu as pltpu
from jax.sharding import PartitionSpec as P

F32 = jnp.float32
BF16 = jnp.bfloat16
LOG2E = 1.4426950408889634
LN2 = 0.6931471805599453
T = 128
E = 2048
N = 16
RANK = 64
KT = E // 128
S = 8
L = T // S
COLS = RANK + 2 * N
ROWS_D = 128
ROWS_X = 64
HALF_D = ROWS_D // 2
HALF_X = ROWS_X // 2
MESH = pl.DeviceIdType.MESH
VMEM = pl.BlockSpec(memory_space=pltpu.VMEM)
ANY = pl.BlockSpec(memory_space=pl.ANY)
SMEM = pl.BlockSpec(memory_space=pltpu.SMEM)


def lanes(k):
    return pl.ds(pl.multiple_of(k * 128, 128), 128)


def store_permuted(ref, k, value):
    for blk in range(T // 8):
        first = (blk % 2) * 64 + blk // 2
        ref[k, pl.ds(first, 8, stride=8), :] = value[blk * 8 : blk * 8 + 8, :]


def load_natural(ref, k):
    parts = []
    for blk in range(T // 8):
        first = (blk % 2) * 64 + blk // 2
        parts.append(ref[k, pl.ds(first, 8, stride=8), :])
    return jnp.concatenate(parts, axis=0)


def sigmoid(v):
    return 1.0 / (1.0 + jnp.exp(-v))


def softplus(v):
    z = jnp.exp(-jnp.abs(v))
    r = z / (z + 2.0)
    q = r * r
    poly = 1.0 / 15.0
    for odd in (13.0, 11.0, 9.0, 7.0, 5.0, 3.0, 1.0):
        poly = poly * q + 1.0 / odd
    return jnp.maximum(v, 0.0) + 2.0 * r * poly


def live_mask(len_ref):
    t0 = lax.axis_index("seq") * T
    pos = t0 + lax.broadcasted_iota(jnp.int32, (T, 128), 0)
    return (pos < len_ref[0]).astype(F32)


def fid_row(lab_ref, fid_ref, ls):
    label = lab_ref[0]
    row = jnp.zeros((1, 128), F32)
    for kind in range(2):
        row = row + jnp.where(label == kind, fid_ref[kind : kind + 1, ls], 0.0)
    return row


def row8(ref, n, ls):
    return jnp.broadcast_to(ref[n : n + 1, ls], (8, 128))


def tile8(n):
    return pl.ds(pl.multiple_of(n * S, S), S)


def step_kernel(
    len_ref, lab_ref, u_hbm, gate_hbm, gg_hbm, xp_hbm, dtp_hbm, dtb_hbm, fid_hbm, al_hbm, skip_hbm,
    gated_hbm, gin_hbm, ggate_hbm, tot_d, tot_x,
    u_ref, gate_ref, gg_ref, xp_ref, dtp_ref, dtb_ref, fid_ref, al_ref, skip_ref, a2_ref, a2w,
    low_ref, step_ref, su_ref, gy_ref, bb_ref, cb_ref, segs_ref, hs_ref, as_ref,
    send_h, send_a, got_h, got_a, back_h, back_a, st_h, st_a,
    hbuf, bgr, cgr, ybuf, sbuf, gbuf, agbuf, dtg, dirs, sl_ref, zg_ref, ds_ref,
    gated_ref, gin_ref, ggate_ref, bcg_ref,
    grads_d, pair_d, part_d, peers_d, mine_d, zparts_d, grads_x, pair_x, part_x, peers_x, mine_x, zparts_x,
    in_sems, out_sems, x_send, x_recv, pair_send, pair_recv, chip_send, chip_recv,
    z_send, z_recv, fin_send, fin_recv, all_send, all_recv,
):
    chips = lax.axis_size("dp")
    size = lax.axis_size("seq")
    depth = size // 2
    dp = lax.axis_index("dp")
    me = lax.axis_index("seq")
    z = me // 2
    core = lax.rem(me, 2)
    sib = me + 1 - 2 * core

    loads = []
    pairs = (
        (u_hbm.at[0], u_ref), (xp_hbm, xp_ref), (dtp_hbm, dtp_ref), (dtb_hbm, dtb_ref), (fid_hbm, fid_ref),
        (gate_hbm.at[0], gate_ref), (gg_hbm.at[0], gg_ref), (al_hbm, al_ref), (skip_hbm, skip_ref),
    )
    for i, (src, dst) in enumerate(pairs):
        copy = pltpu.make_async_copy(src, dst, in_sems.at[i])
        copy.start()
        loads.append(copy)

    barrier = pltpu.get_barrier_semaphore()
    for o in range(1, chips):
        d = lax.rem(dp + o, chips)
        pl.semaphore_signal(barrier, inc=1, device_id={"dp": d}, device_id_type=MESH)
    for o in range(1, size):
        j = lax.rem(me + o, size)
        pl.semaphore_signal(barrier, inc=1, device_id={"seq": j}, device_id_type=MESH)

    def remote(src, dst, send, recv, where):
        return pltpu.make_async_remote_copy(
            src_ref=src, dst_ref=dst, send_sem=send, recv_sem=recv, device_id=where, device_id_type=MESH
        )

    def hop(which, src, dst, j, slot):
        return remote(src.at[j], dst.at[slot], x_send.at[which, j], x_recv.at[which, slot], {"seq": j})

    def there_h(j, slot):
        return hop(0, send_h, got_h, j, slot)

    def there_a(j, slot):
        return hop(1, send_a, got_a, j, slot)

    def home_h(j, slot):
        return hop(2, back_h, st_h, j, slot)

    def home_a(j, slot):
        return hop(3, back_a, st_a, j, slot)

    def group(g):
        return [2 * lax.rem(z + o, depth) + g for o in range(1, depth)]

    def send_group(copy, g, src, dst):
        for j in group(g):
            copy(j, me).start()

        @pl.when(core != g)
        def _():
            copy(sib, me).start()

        @pl.when(core == g)
        def _():
            dst[pl.ds(me, 1)] = src[pl.ds(me, 1)]

    def wait_group(copy, g):
        for j in group(g):
            copy(j, j).wait_recv()

        @pl.when(core != g)
        def _():
            copy(sib, sib).wait_recv()

    grads, pair, part = (grads_d, grads_x), (pair_d, pair_x), (part_d, part_x)
    peers, mine, zparts = (peers_d, peers_x), (mine_d, mine_x), (zparts_d, zparts_x)
    halves = (HALF_D, HALF_X)

    def half_of(p, c):
        return pl.ds(pl.multiple_of(c * halves[p], 8), halves[p])

    def to_sib(p, d):
        return remote(
            grads[p].at[d, half_of(p, 1 - core)], pair[p].at[d],
            pair_send.at[p, d], pair_recv.at[p, d], {"seq": sib},
        )

    def to_chip(p, d, slot):
        return remote(
            part[p].at[d], peers[p].at[slot], chip_send.at[p, d], chip_recv.at[p, slot], {"dp": d}
        )

    def to_level(p, q, slot):
        src = mine_x if p else mine_d.at[pl.ds(pl.multiple_of(q * 8, 8), 8)]
        return remote(
            src, zparts[p].at[slot], z_send.at[p, q], z_recv.at[p, slot], {"seq": q * 2 + core}
        )

    def gather_d(j, c, q):
        here = tot_d.at[pl.ds(pl.multiple_of(c * HALF_D + q * 8, 8), 8)]
        return remote(here, here, all_send.at[j], all_recv.at[2 * q + c], {"seq": j})

    def last(c):
        here = tot_x.at[half_of(1, c)]
        return remote(here, here, fin_send.at[0], fin_recv.at[0], {"seq": sib})

    loads[0].wait()
    loads[1].wait()
    proj = lax.dot_general(
        u_ref[...], xp_ref[...], (((1,), (1,)), ((), ())), preferred_element_type=F32
    )
    low_ref[...] = proj[:, :RANK].astype(BF16)
    for n in range(N):
        for col, ref in ((RANK + n, bb_ref), (RANK + N + n, cb_ref)):
            wide = jnp.broadcast_to(proj[:, col : col + 1], (T, 128))
            for blk in range(T // 8):
                first = (blk % 2) * 8 * (N * S) + n * S + blk // 2
                ref[pl.ds(first, 8, stride=N * S), :] = wide[blk * 8 : blk * 8 + 8, :]
    for copy in loads[2:]:
        copy.wait()
    a2_ref[...] = -LOG2E * jnp.exp(al_ref[...])
    live = live_mask(len_ref)

    def dt_before(ls):
        return (
            jnp.dot(low_ref[...], dtp_ref[:, ls], preferred_element_type=F32)
            + dtb_ref[:, ls]
            + fid_row(lab_ref, fid_ref, ls)
        )

    @pl.loop(0, KT // 2)
    def _(turn):
        ks = [turn * 2 + q for q in range(2)]
        raws = [dt_before(lanes(k)) for k in ks]
        for k, dt_raw in zip(ks, raws):
            ls = lanes(k)
            step = softplus(dt_raw) * live
            u = u_ref[:, ls].astype(F32)
            store_permuted(step_ref, k, step)
            store_permuted(su_ref, k, step * u)
            for n in range(N):
                a2w[k, n * S : n * S + S, :] = row8(a2_ref, n, ls)

    GK = 2
    PAIRS = KT // GK

    def tiles_of(g, q):
        return [4 * q + g, 4 * q + 2 + g]

    def zero_ends(g):
        @pl.loop(0, PAIRS // 2)
        def _(q):
            ks = tiles_of(g, q)
            GN = 8

            @pl.loop(0, N // GN)
            def _(ng):
                ns = [ng * GN + j for j in range(GN)]
                a2 = [[a2w[k, tile8(n), :] for k in ks] for n in ns]

                def ahead(tau, hh):
                    rows = tile8(tau)
                    st = [step_ref[k, rows, :] for k in ks]
                    su = [su_ref[k, rows, :] for k in ks]
                    out = []
                    for j, n in enumerate(ns):
                        b = bb_ref[tile8(tau * N + n), :]
                        for i in range(GK):
                            out.append(jnp.exp2(a2[j][i] * st[i]) * hh[j * GK + i] + b * su[i])
                    return tuple(out)

                zero = jnp.zeros((S, 128), F32)
                ends = lax.fori_loop(0, L, ahead, (zero,) * (GN * GK), unroll=16)
                for j, n in enumerate(ns):
                    for i, k in enumerate(ks):
                        hs_ref[k, tile8(n), :] = ends[j * GK + i]

        @pl.loop(0, KT // 2)
        def _(q):
            k = 2 * q + g
            seg = step_ref[k, pl.ds(0, S), :]
            for tau in range(1, L):
                seg = seg + step_ref[k, pl.ds(tau * S, S), :]
            segs_ref[k] = seg
            for nh in range(2):
                a2 = a2_ref[nh * 8 : nh * 8 + 8, lanes(k)]
                h = hs_ref[k, pl.ds(nh * 64, 8, stride=8), :]
                for s in range(1, S):
                    h = jnp.exp2(a2 * seg[s : s + 1, :]) * h + hs_ref[k, pl.ds(nh * 64 + s, 8, stride=8), :]
                send_h[k, pl.ds(nh * 8, 8), :] = h
            total = jnp.sum(seg, axis=0, keepdims=True)
            send_h[k, pl.ds(16, 8), :] = jnp.broadcast_to(total, (8, 128))

    zero_ends(0)
    pl.semaphore_wait(barrier, chips + size - 2)
    send_group(there_h, 0, send_h, got_h)
    zero_ends(1)
    send_group(there_h, 1, send_h, got_h)

    @pl.loop(0, KT // 2)
    def _(turn):
        for q in range(2):
            k = turn * 2 + q
            ls = lanes(k)
            gate = gate_ref[:, ls].astype(F32)
            sig = sigmoid(gate)
            silu = gate * sig * live
            gg = gg_ref[:, ls].astype(F32)
            sl_ref[:, ls] = silu
            zg_ref[:, ls] = gg * live * (sig * (1.0 + gate * (1.0 - sig)))
            store_permuted(gy_ref, k, gg * silu)

    def zero_pulls(g):
        @pl.loop(0, PAIRS // 2)
        def _(q):
            ks = tiles_of(g, q)
            GN = 4

            @pl.loop(0, N // GN)
            def _(ng):
                ns = [ng * GN + j for j in range(GN)]
                a2 = [[a2w[k, tile8(n), :] for k in ks] for n in ns]

                def pull(tau, state):
                    rows = tile8(tau)
                    cum = [state[i] + step_ref[k, rows, :] for i, k in enumerate(ks)]
                    gy = [gy_ref[k, rows, :] for k in ks]
                    out = list(cum)
                    for j, n in enumerate(ns):
                        c = cb_ref[tile8(tau * N + n), :]
                        for i in range(GK):
                            acc = state[GK + j * GK + i]
                            out.append(acc + jnp.exp2(a2[j][i] * cum[i]) * (c * gy[i]))
                    return tuple(out)

                zero = jnp.zeros((S, 128), F32)
                ends = lax.fori_loop(0, L, pull, (zero,) * (GK + GN * GK), unroll=16)
                for j, n in enumerate(ns):
                    for i, k in enumerate(ks):
                        as_ref[k, tile8(n), :] = ends[GK + j * GK + i]

        @pl.loop(0, KT // 2)
        def _(q):
            k = 2 * q + g
            for nh in range(2):
                a2 = a2_ref[nh * 8 : nh * 8 + 8, lanes(k)]
                h = as_ref[k, pl.ds(nh * 64 + S - 1, 8, stride=8), :]
                for s in range(S - 2, -1, -1):
                    p = jnp.exp2(a2 * segs_ref[k, s : s + 1, :])
                    h = p * h + as_ref[k, pl.ds(nh * 64 + s, 8, stride=8), :]
                send_a[k, pl.ds(nh * 8, 8), :] = h

    zero_pulls(0)
    send_group(there_a, 0, send_a, got_a)
    zero_pulls(1)
    send_group(there_a, 1, send_a, got_a)

    bgr[...] = jnp.zeros_like(bgr)
    cgr[...] = jnp.zeros_like(cgr)

    a2_mine = a2_ref[:, lanes(me)]
    for o in range(1, size):
        j = lax.rem(me + o, size)
        there_h(j, j).wait_recv()
    h = jnp.zeros((N, 128), F32)
    for i in range(size):
        back_h[i] = h
        h = jnp.exp2(a2_mine * got_h[i, 16:17, :]) * h + got_h[i, 0:16, :]
    for o in range(1, size):
        home_h(lax.rem(me + o, size), me).start()
    st_h[pl.ds(me, 1)] = back_h[pl.ds(me, 1)]

    @pl.loop(0, KT // 4)
    def _(turn):
        ks = [turn * 4 + q for q in range(4)]
        raws = [dt_before(lanes(k)) for k in ks]
        for k, dt_raw in zip(ks, raws):
            ds_ref[:, lanes(k)] = live * sigmoid(dt_raw)

    for o in range(1, size):
        j = lax.rem(me + o, size)
        there_a(j, j).wait_recv()
    g = jnp.zeros((N, 128), F32)
    for i in range(size - 1, -1, -1):
        back_a[i] = g
        g = jnp.exp2(a2_mine * got_h[i, 16:17, :]) * g + got_a[i]
    for o in range(1, size):
        home_a(lax.rem(me + o, size), me).start()
    st_a[pl.ds(me, 1)] = back_a[pl.ds(me, 1)]

    def full_forward(g):
        wait_group(home_h, g)

        @pl.loop(0, KT // 2)
        def _(q):
            k = 2 * q + g
            for nh in range(2):
                a2 = a2_ref[nh * 8 : nh * 8 + 8, lanes(k)]
                h = st_h[k, nh * 8 : nh * 8 + 8, :]
                for s in range(S):
                    at = pl.ds(nh * 64 + s, 8, stride=8)
                    end = hs_ref[k, at, :]
                    hs_ref[k, at, :] = h
                    if s + 1 < S:
                        h = jnp.exp2(a2 * segs_ref[k, s : s + 1, :]) * h + end

        @pl.loop(0, PAIRS // 2)
        def _(q):
            ks = tiles_of(g, q)
            kp = g * (PAIRS // 2) + q
            FN = 8
            for ng in range(N // FN):
                ns = [ng * FN + j for j in range(FN)]
                a2 = [[a2w[k, n * S : n * S + S, :] for k in ks] for n in ns]
                first = []
                for n in ns:
                    for i, k in enumerate(ks):
                        h = hs_ref[k, n * S : n * S + S, :]
                        hbuf[kp * (L + 1) * N * GK + n * GK + i] = h
                        first.append(h)

                def forward(tau, hh):
                    rows = tile8(tau)
                    st = [step_ref[k, rows, :] for k in ks]
                    su = [su_ref[k, rows, :] for k in ks]
                    gy = [gy_ref[k, rows, :] for k in ks]
                    ys = [None] * GK
                    out = []
                    for j, n in enumerate(ns):
                        at = tile8(tau * N + n)
                        b = bb_ref[at, :]
                        c = cb_ref[at, :]
                        cg = None
                        for i in range(GK):
                            h = jnp.exp2(a2[j][i] * st[i]) * hh[j * GK + i] + b * su[i]
                            out.append(h)
                            hbuf[(kp * (L + 1) + tau + 1) * (N * GK) + n * GK + i] = h
                            term = c * h
                            ys[i] = term if ys[i] is None else ys[i] + term
                            term = h * gy[i]
                            cg = term if cg is None else cg + term
                        cgr[at, :] = cgr[at, :] + cg
                    for i, k in enumerate(ks):
                        if ng == 0:
                            ybuf[k, rows, :] = ys[i]
                        else:
                            ybuf[k, rows, :] = ybuf[k, rows, :] + ys[i]
                    return tuple(out)

                lax.fori_loop(0, L, forward, tuple(first), unroll=16)

    full_forward(0)
    full_forward(1)

    def full_backward(g):
        wait_group(home_a, g)

        @pl.loop(0, KT // 2)
        def _(q):
            k = 2 * q + g
            for nh in range(2):
                a2 = a2_ref[nh * 8 : nh * 8 + 8, lanes(k)]
                h = st_a[k, nh * 8 : nh * 8 + 8, :]
                for s in range(S - 1, -1, -1):
                    at = pl.ds(nh * 64 + s, 8, stride=8)
                    end = as_ref[k, at, :]
                    as_ref[k, at, :] = h
                    if s > 0:
                        h = jnp.exp2(a2 * segs_ref[k, s : s + 1, :]) * h + end

        @pl.loop(0, PAIRS // 2)
        def _(q):
            ks = tiles_of(g, q)
            kp = g * (PAIRS // 2) + q
            BN = 4
            for ng in range(N // BN):
                ns = [ng * BN + j for j in range(BN)]
                a2 = [[a2w[k, n * S : n * S + S, :] for k in ks] for n in ns]
                carry = [as_ref[k, n * S : n * S + S, :] for n in ns for k in ks]
                zero = jnp.zeros((S, 128), F32)

                def behind(turn, state):
                    tau = L - 1 - turn
                    cs, ags = state
                    rows = tile8(tau)
                    st = [step_ref[k, rows, :] for k in ks]
                    su = [su_ref[k, rows, :] for k in ks]
                    gy = [gy_ref[k, rows, :] for k in ks]
                    sb = [None] * GK
                    sg = [None] * GK
                    new_c, new_a = [], []
                    for j, n in enumerate(ns):
                        at = tile8(tau * N + n)
                        b = bb_ref[at, :]
                        c = cb_ref[at, :]
                        bg = None
                        for i in range(GK):
                            g = c * gy[i] + cs[j * GK + i]
                            term = g * b
                            sb[i] = term if sb[i] is None else sb[i] + term
                            term = g * su[i]
                            bg = term if bg is None else bg + term
                            dg = jnp.exp2(a2[j][i] * st[i]) * g
                            w = dg * hbuf[(kp * (L + 1) + tau) * (N * GK) + n * GK + i]
                            term = a2[j][i] * w
                            sg[i] = term if sg[i] is None else sg[i] + term
                            new_c.append(dg)
                            new_a.append(ags[j * GK + i] + st[i] * w)
                        bgr[at, :] = bgr[at, :] + bg
                    for i, k in enumerate(ks):
                        if ng == 0:
                            sbuf[k, rows, :] = sb[i]
                            gbuf[k, rows, :] = sg[i]
                        else:
                            sbuf[k, rows, :] = sbuf[k, rows, :] + sb[i]
                            gbuf[k, rows, :] = gbuf[k, rows, :] + sg[i]
                    return tuple(new_c), tuple(new_a)

                _, ags = lax.fori_loop(0, L, behind, (tuple(carry), (zero,) * (BN * GK)), unroll=16)
                for j, n in enumerate(ns):
                    for i, k in enumerate(ks):
                        agbuf[k, n * S : n * S + S, :] = ags[j * GK + i]

    full_backward(0)
    full_backward(1)

    label = lab_ref[0]
    lane = lax.broadcasted_iota(jnp.int32, (128, 128), 1)
    sums = jnp.zeros((T, 128), F32)
    for n in range(N):
        for col, ref in ((n, bgr), (N + n, cgr)):
            tile = jnp.concatenate(
                [ref[(tau * N + n) * S : (tau * N + n) * S + S, :] for tau in range(L)], axis=0
            )
            hi = tile.astype(BF16)
            lo = (tile - hi.astype(F32)).astype(BF16)
            pick = (lane == col).astype(BF16)
            sums = sums + jnp.dot(hi, pick, preferred_element_type=F32)
            sums = sums + jnp.dot(lo, pick, preferred_element_type=F32)
    dirs[0] = sums
    bcg_ref[...] = load_natural(dirs, 0)[:, : 2 * N].astype(BF16)

    def pass_on(p, i):
        d = lax.rem(dp + 1 + i, chips)
        to_sib(p, d).wait_recv()
        part[p][pl.ds(d, 1)] = grads[p][pl.ds(d, 1), half_of(p, core)] + pair[p][pl.ds(d, 1)]

    def send_on(p, i):
        pass_on(p, i)
        to_chip(p, lax.rem(dp + 1 + i, chips), dp).start()

    def early_block(i):
        k = lax.rem(dp + 1 + i, chips)
        ls = lanes(k)
        u = u_ref[:, ls]
        uf = u.astype(F32)
        step_grad = LN2 * load_natural(gbuf, k) + uf * load_natural(sbuf, k)
        dt_grad = step_grad * ds_ref[:, ls]
        dt_b = dt_grad.astype(BF16)
        dtg[:, ls] = dt_b
        grads_d[k, 0:RANK, :] = lax.dot_general(
            low_ref[...], dt_b, (((0,), (0,)), ((), ())), preferred_element_type=F32
        )
        for nh in range(2):
            ag = agbuf[k, pl.ds(nh * 64, 8, stride=8), :]
            for s in range(1, S):
                ag = ag + agbuf[k, pl.ds(nh * 64 + s, 8, stride=8), :]
            grads_d[k, RANK + nh * 8 : RANK + nh * 8 + 8, :] = (
                ag * a2_ref[nh * 8 : nh * 8 + 8, ls] * LN2
            )
        skip_row = jnp.sum(gg_ref[:, ls].astype(F32) * sl_ref[:, ls] * uf, axis=0, keepdims=True)
        dt_row = jnp.sum(dt_grad, axis=0, keepdims=True)
        zero = jnp.zeros_like(dt_row)
        base = RANK + N
        grads_d[k, base : base + 8, :] = jnp.concatenate(
            [
                skip_row,
                dt_row,
                jnp.where(label == 0, dt_row, zero),
                jnp.where(label == 1, dt_row, zero),
                zero, zero, zero, zero,
            ],
            axis=0,
        )
        grads_d[k, base + 8 : base + 8 + 2 * N, :] = lax.dot_general(
            bcg_ref[...], u, (((0,), (0,)), ((), ())), preferred_element_type=F32
        )
        grads_d[k, base + 8 + 2 * N : ROWS_D, :] = jnp.zeros((ROWS_D - base - 8 - 2 * N, 128), F32)
        return k

    def early_turn(turn):
        made = [early_block(turn * 2 + q) for q in range(2)]
        for k in made:
            to_sib(0, k).start()

    early_turn(0)

    @pl.loop(1, KT // 2)
    def _(turn):
        early_turn(turn)
        send_on(0, turn * 2 - 2)
        send_on(0, turn * 2 - 1)

    low_grad = lax.dot_general(
        dtg[...], dtp_ref[...], (((1,), (1,)), ((), ())), preferred_element_type=F32
    ).astype(BF16)
    send_on(0, KT - 2)
    pass_on(0, KT - 1)

    def late_turn(turn):
        made = [lax.rem(dp + 1 + turn * 4 + q, chips) for q in range(4)]
        for k in made:
            grads_x[k] = lax.dot_general(
                low_grad, u_ref[:, lanes(k)], (((0,), (0,)), ((), ())), preferred_element_type=F32
            )
        for k in made:
            to_sib(1, k).start()

    late_turn(0)

    @pl.loop(1, KT // 4)
    def _(turn):
        late_turn(turn)
        for q in range(4):
            send_on(1, turn * 4 - 4 + q)

    for q in range(3):
        send_on(1, KT - 4 + q)
    pass_on(1, KT - 1)

    def add_up(p):
        total = part[p][dp]
        for o in range(1, chips):
            d = lax.rem(dp + chips - o, chips)
            to_chip(p, d, d).wait_recv()
            total = total + peers[p][d]
        mine[p][...] = total
        for o in range(1, depth):
            to_level(p, lax.rem(z + o, depth), z).start()

    @pl.loop(0, KT // 2)
    def _(turn):
        for q in range(2):
            k = turn * 2 + q
            ls = lanes(k)
            y = load_natural(ybuf, k) + skip_ref[:, ls] * u_ref[:, ls].astype(F32)
            gated_ref[:, ls] = (y * sl_ref[:, ls]).astype(BF16)
            ggate_ref[:, ls] = (y * zg_ref[:, ls]).astype(BF16)

    out_gated = pltpu.make_async_copy(gated_ref, gated_hbm.at[0], out_sems.at[0])
    out_gated.start()
    out_ggate = pltpu.make_async_copy(ggate_ref, ggate_hbm.at[0], out_sems.at[1])
    out_ggate.start()
    add_up(0)
    proj_grad = jnp.concatenate([low_grad, bcg_ref[...]], axis=1)

    @pl.loop(0, KT // 2)
    def _(turn):
        for q in range(2):
            k = turn * 2 + q
            ls = lanes(k)
            back = jnp.dot(proj_grad, xp_ref[:, ls], preferred_element_type=F32)
            direct = load_natural(step_ref, k) * load_natural(sbuf, k)
            straight = gg_ref[:, ls].astype(F32) * sl_ref[:, ls] * skip_ref[:, ls]
            gin_ref[:, ls] = (direct + straight + back).astype(BF16)

    out_gin = pltpu.make_async_copy(gin_ref, gin_hbm.at[0], out_sems.at[2])
    out_gin.start()
    add_up(1)
    total = mine_d[pl.ds(pl.multiple_of(z * 8, 8), 8)]
    for o in range(1, depth):
        q = lax.rem(z + o, depth)
        to_level(0, q, q).wait_recv()
        total = total + zparts_d[q]
    tot_d[pl.ds(pl.multiple_of(core * HALF_D + z * 8, 8), 8)] = total
    for o in range(1, size):
        gather_d(lax.rem(me + o, size), core, z).start()
    total = mine_x[...]
    for o in range(1, depth):
        q = lax.rem(z + o, depth)
        to_level(1, q, q).wait_recv()
        total = total + zparts_x[q]
    tot_x[half_of(1, core), :] = total
    last(core).start()
    for o in range(1, size):
        j = lax.rem(me + o, size)
        gather_d(j, lax.rem(j, 2), j // 2).wait_recv()
    last(1 - core).wait_recv()

    for o in range(1, size):
        j = lax.rem(me + o, size)
        there_h(j, me).wait_send()
        there_a(j, me).wait_send()
        home_h(j, me).wait_send()
        home_a(j, me).wait_send()
    last(core).wait_send()
    for o in range(1, size):
        gather_d(lax.rem(me + o, size), core, z).wait_send()
    for p in range(2):
        for d in range(chips):
            to_sib(p, d).wait_send()
        for o in range(1, chips):
            to_chip(p, lax.rem(dp + o, chips), dp).wait_send()
        for o in range(1, depth):
            to_level(p, lax.rem(z + o, depth), z).wait_send()
    out_gated.wait()
    out_ggate.wait()
    out_gin.wait()


def finish(
    gated_in, gin_in, ggate_in, tot_d, tot_x,
    gated_out, gin_out, ggate_out, gx_ref, gdt_ref, ga_ref, gs_ref, gb_ref, gf_ref,
    hold, in_sems, out_sems,
):
    chunks = 2
    rows = T // chunks
    ins, outs = [], []
    for i, (src, dst) in enumerate(
        ((gated_in, gated_out), (gin_in, gin_out), (ggate_in, ggate_out))
    ):
        for q in range(chunks):
            at = pl.ds(q * rows, rows)
            one = i * chunks + q
            ins.append(pltpu.make_async_copy(src.at[0, at], hold.at[i, at], in_sems.at[one]))
            outs.append(pltpu.make_async_copy(hold.at[i, at], dst.at[0, at], out_sems.at[one]))
    for copy in ins:
        copy.start()
    base = RANK + N
    gx_ref[0:RANK, :] = tot_x[...]
    gx_ref[RANK:COLS, :] = tot_d[base + 8 : base + 8 + 2 * N, :]
    gdt_ref[...] = tot_d[0:RANK, :]
    ga_ref[...] = tot_d[RANK:base, :]
    gs_ref[...] = tot_d[base : base + 1, :]
    gb_ref[...] = tot_d[base + 1 : base + 2, :]
    gf_ref[...] = tot_d[base + 2 : base + 4, :]
    for into, out in zip(ins, outs):
        into.wait()
        out.start()
    for out in outs:
        out.wait()


def sds(shape, dtype=F32):
    return jax.ShapeDtypeStruct(shape, dtype)


def vm(shape, dtype=F32):
    return pltpu.VMEM(shape, dtype)


def call_step(*operands):
    dma = pltpu.SemaphoreType.DMA
    big = sds((1, T, E), BF16)
    return pl.pallas_call(
        step_kernel,
        out_shape=(big, big, big, sds((ROWS_D, 128)), sds((ROWS_X, 128))),
        in_specs=[SMEM, SMEM] + [ANY] * 9,
        out_specs=(ANY, ANY, ANY, VMEM, VMEM),
        scratch_shapes=[
            vm((T, E), BF16), vm((T, E), BF16), vm((T, E), BF16), vm((COLS, E), BF16), vm((RANK, E), BF16),
            vm((1, E)), vm((2, E)), vm((N, E)), vm((1, E)), vm((N, E)), vm((KT, N * S, 128)),
            vm((T, RANK), BF16), vm((KT, T, 128)), vm((KT, T, 128)), vm((KT, T, 128)),
            vm((L * N * S, 128)), vm((L * N * S, 128)), vm((KT, S, 128)),
            vm((KT, N * S, 128)), vm((KT, N * S, 128)),
            vm((16, 24, 128)), vm((16, 16, 128)), vm((16, 24, 128)), vm((16, 16, 128)),
            vm((16, 16, 128)), vm((16, 16, 128)), vm((16, 16, 128)), vm((16, 16, 128)),
            vm((KT * (L + 1) * N, S, 128)), vm((L * N * S, 128)), vm((L * N * S, 128)),
            vm((KT, T, 128)), vm((KT, T, 128)), vm((KT, T, 128)), vm((KT, N * S, 128)),
            vm((T, E), BF16), vm((1, T, 128)), vm((T, E)), vm((T, E)), vm((T, E)),
            vm((T, E), BF16), vm((T, E), BF16), vm((T, E), BF16),
            vm((T, 2 * N), BF16),
            vm((16, ROWS_D, 128)), vm((16, HALF_D, 128)), vm((16, HALF_D, 128)), vm((16, HALF_D, 128)),
            vm((HALF_D, 128)), vm((8, 8, 128)),
            vm((16, ROWS_X, 128)), vm((16, HALF_X, 128)), vm((16, HALF_X, 128)), vm((16, HALF_X, 128)),
            vm((HALF_X, 128)), vm((8, HALF_X, 128)),
            dma((9,)), dma((3,)), dma((4, 16)), dma((4, 16)), dma((2, 16)), dma((2, 16)),
            dma((2, 16)), dma((2, 16)), dma((2, 8)), dma((2, 8)), dma((1,)), dma((1,)),
            dma((16,)), dma((16,)),
        ],
        compiler_params=pltpu.CompilerParams(
            collective_id=0, has_side_effects=True, vmem_limit_bytes=60 << 20
        ),
        name="step_kernel",
    )(*operands)


def call_finish(*operands):
    big = sds((1, T, E), BF16)
    return pl.pallas_call(
        finish,
        out_shape=(
            big, big, big, sds((COLS, 128)), sds((RANK, 128)), sds((N, 128)), sds((1, 128)),
            sds((1, 128)), sds((2, 128)),
        ),
        in_specs=[ANY, ANY, ANY, VMEM, VMEM],
        out_specs=(ANY, ANY, ANY) + (VMEM,) * 6,
        scratch_shapes=[
            vm((3, T, E), BF16), pltpu.SemaphoreType.DMA((6,)), pltpu.SemaphoreType.DMA((6,)),
        ],
        name="finish",
    )(*operands)


def per_device(
    ssm_input, gate_input, grad_gated, x_proj, dt_proj, dt_bias, fid_bias, a_log, skip_gain,
    rec_lengths, fid_labels,
):
    results = call_step(
        rec_lengths, fid_labels, ssm_input, gate_input, grad_gated, x_proj.T, dt_proj,
        dt_bias[None, :], fid_bias, a_log.T, skip_gain[None, :],
    )
    gated, gin, ggate, gx, gdt, ga, gs, gb, gf = call_finish(*results)
    return (gated, gin, ggate, gx.T, gdt, ga.T, gs[0], gb[0], gf)


def solution(mesh):
    wide = P("dp", "seq", None)
    in_specs = (wide, wide, wide, P(), P(), P(), P(), P(), P(), P("dp"), P("dp"))
    out_specs = (
        wide, wide, wide, P("dp", None), P(None, "dp"), P("dp", None), P("dp"), P("dp"), P(None, "dp"),
    )
    return jax.shard_map(
        per_device, mesh=mesh, in_specs=in_specs, out_specs=out_specs, check_vma=False
    )
```

time: 86.7 us -> 73.6 us (0.85); the launches traced: 86.5 us -> 72.3 us
  Pallas kernels: 84.6 us -> 70.3 us
    pallas_call x1, Pallas kernels: 80.8 us -> 66.7 us  [call_step(): pl.pallas_call(step_kernel, out_shape=(big, big, big, sds((ROWS_D, 128)),...]
where the time goes in v3:
time: 73.6 us; the launch traced here: 72.3 us
  Pallas kernels  70.3 us (96%)
  between operations  1.95 us (3%)
    pallas_call x1, Pallas kernels, call_step(): pl.pallas_call(step_kernel, out_shape=(big, big, big, sds((ROWS_D, 128)),...  66.7 us
    pallas_call x1, Pallas kernels, call_finish(): pl.pallas_call(finish, out_shape=(big, big, big, sds((COLS, 128)), sds((R...  3.67 us

profile of v3, /device:TPU:1, one launch (start us, length us, event | category | flops | bytes accessed | tf_op | source)
XLA Modules:
  0.0 72.3 jit_solution(8004705954884412814)
XLA Ops:
  1.9 66.7 %step_kernel.1 = (bf16[1,128,2048]{2,1,0:T(8,128)(2,1)}, bf16[1,128,2048]{2,1,0:T(8,128)(2,1)}, bf16[1,128,2048]{2,1,0:T(8,128)(2,1)}, f32[128,128]{1,0:T(8,128)}, f32[64,128]{1,0:T(8,128)}) custom-call(s32[1]{0:T(128)S(6)} %copy.20.len_ref, s32[1]{0:T(128)S(6)} %copy.21.lab_ref, bf16[1,128,2048]{2,1,0:T(8,128)(2,1)} %u_hbm.1, ...), custom_call_target="tpu_custom_call" | custom-call | tf_op jit(solution)/shard_map/step_kernel/pallas_call | solution.py:746
  68.6 3.7 %finish.1 = (bf16[1,128,2048]{2,1,0:T(8,128)(2,1)}, bf16[1,128,2048]{2,1,0:T(8,128)(2,1)}, bf16[1,128,2048]{2,1,0:T(8,128)(2,1)}, f32[96,128]{1,0:T(8,128)}, f32...) custom-call(bf16[1,128,2048]{2,1,0:T(8,128)(2,1)} %get-tuple-element.23.gated, ...), custom_call_target="tpu_custom_call" | custom-call | tf_op jit(solution)/shard_map/finish/pallas_call | solution.py:781

commit v4 on v3

--- a/solution.py
+++ b/solution.py
@@ -126,7 +126,12 @@
         )
 
     def hop(which, src, dst, j, slot):
-        return remote(src.at[j], dst.at[slot], x_send.at[which, j], x_recv.at[which, slot], {"seq": j})
+        kind = which if which < 2 else 2 * which - 2 + core
+        return remote(src.at[j], dst.at[slot], x_send.at[which], x_recv.at[kind], {"seq": j})
+
+    def bulk(ref, count, send, recv):
+        some = ref.at[pl.ds(0, count)]
+        return remote(some, some, send, recv, {"seq": sib})
 
     def there_h(j, slot):
         return hop(0, send_h, got_h, j, slot)
@@ -155,13 +160,14 @@
         def _():
             dst[pl.ds(me, 1)] = src[pl.ds(me, 1)]
 
-    def wait_group(copy, g):
-        for j in group(g):
-            copy(j, j).wait_recv()
-
+    def wait_group(which, dst, g):
         @pl.when(core != g)
         def _():
-            copy(sib, sib).wait_recv()
+            bulk(dst, depth, x_send.at[which], x_recv.at[2 * which - 2 + g]).wait_recv()
+
+        @pl.when(core == g)
+        def _():
+            bulk(dst, depth - 1, x_send.at[which], x_recv.at[2 * which - 2 + g]).wait_recv()
 
     grads, pair, part = (grads_d, grads_x), (pair_d, pair_x), (part_d, part_x)
     peers, mine, zparts = (peers_d, peers_x), (mine_d, mine_x), (zparts_d, zparts_x)
@@ -170,26 +176,26 @@
     def half_of(p, c):
         return pl.ds(pl.multiple_of(c * halves[p], 8), halves[p])
 
-    def to_sib(p, d):
+    def to_sib(p, d, turn):
         return remote(
             grads[p].at[d, half_of(p, 1 - core)], pair[p].at[d],
-            pair_send.at[p, d], pair_recv.at[p, d], {"seq": sib},
+            pair_send.at[p], pair_recv.at[p, turn], {"seq": sib},
         )
 
     def to_chip(p, d, slot):
         return remote(
-            part[p].at[d], peers[p].at[slot], chip_send.at[p, d], chip_recv.at[p, slot], {"dp": d}
+            part[p].at[d], peers[p].at[slot], chip_send.at[p], chip_recv.at[p], {"dp": d}
         )
 
     def to_level(p, q, slot):
         src = mine_x if p else mine_d.at[pl.ds(pl.multiple_of(q * 8, 8), 8)]
         return remote(
-            src, zparts[p].at[slot], z_send.at[p, q], z_recv.at[p, slot], {"seq": q * 2 + core}
+            src, zparts[p].at[slot], z_send.at[p], z_recv.at[p], {"seq": q * 2 + core}
         )
 
     def gather_d(j, c, q):
         here = tot_d.at[pl.ds(pl.multiple_of(c * HALF_D + q * 8, 8), 8)]
-        return remote(here, here, all_send.at[j], all_recv.at[2 * q + c], {"seq": j})
+        return remote(here, here, all_send.at[0], all_recv.at[0], {"seq": j})
 
     def last(c):
         here = tot_x.at[half_of(1, c)]
@@ -350,9 +356,7 @@
     cgr[...] = jnp.zeros_like(cgr)
 
     a2_mine = a2_ref[:, lanes(me)]
-    for o in range(1, size):
-        j = lax.rem(me + o, size)
-        there_h(j, j).wait_recv()
+    bulk(got_h, size - 1, x_send.at[0], x_recv.at[0]).wait_recv()
     h = jnp.zeros((N, 128), F32)
     for i in range(size):
         back_h[i] = h
@@ -368,9 +372,7 @@
         for k, dt_raw in zip(ks, raws):
             ds_ref[:, lanes(k)] = live * sigmoid(dt_raw)
 
-    for o in range(1, size):
-        j = lax.rem(me + o, size)
-        there_a(j, j).wait_recv()
+    bulk(got_a, size - 1, x_send.at[1], x_recv.at[1]).wait_recv()
     g = jnp.zeros((N, 128), F32)
     for i in range(size - 1, -1, -1):
         back_a[i] = g
@@ -380,7 +382,7 @@
     st_a[pl.ds(me, 1)] = back_a[pl.ds(me, 1)]
 
     def full_forward(g):
-        wait_group(home_h, g)
+        wait_group(2, st_h, g)
 
         @pl.loop(0, KT // 2)
         def _(q):
@@ -444,7 +446,7 @@
     full_forward(1)
 
     def full_backward(g):
-        wait_group(home_a, g)
+        wait_group(3, st_a, g)
 
         @pl.loop(0, KT // 2)
         def _(q):
@@ -531,9 +533,11 @@
     dirs[0] = sums
     bcg_ref[...] = load_natural(dirs, 0)[:, : 2 * N].astype(BF16)
 
+    def collect(p, turn):
+        bulk(pair[p], (2, 4)[p], pair_send.at[p], pair_recv.at[p, turn]).wait_recv()
+
     def pass_on(p, i):
         d = lax.rem(dp + 1 + i, chips)
-        to_sib(p, d).wait_recv()
         part[p][pl.ds(d, 1)] = grads[p][pl.ds(d, 1), half_of(p, core)] + pair[p][pl.ds(d, 1)]
 
     def send_on(p, i):
@@ -582,19 +586,21 @@
     def early_turn(turn):
         made = [early_block(turn * 2 + q) for q in range(2)]
         for k in made:
-            to_sib(0, k).start()
+            to_sib(0, k, turn).start()
 
     early_turn(0)
 
     @pl.loop(1, KT // 2)
     def _(turn):
         early_turn(turn)
+        collect(0, turn - 1)
         send_on(0, turn * 2 - 2)
         send_on(0, turn * 2 - 1)
 
     low_grad = lax.dot_general(
         dtg[...], dtp_ref[...], (((1,), (1,)), ((), ())), preferred_element_type=F32
     ).astype(BF16)
+    collect(0, KT // 2 - 1)
     send_on(0, KT - 2)
     pass_on(0, KT - 1)
 
@@ -605,25 +611,27 @@
                 low_grad, u_ref[:, lanes(k)], (((0,), (0,)), ((), ())), preferred_element_type=F32
             )
         for k in made:
-            to_sib(1, k).start()
+            to_sib(1, k, turn).start()
 
     late_turn(0)
 
     @pl.loop(1, KT // 4)
     def _(turn):
         late_turn(turn)
+        collect(1, turn - 1)
         for q in range(4):
             send_on(1, turn * 4 - 4 + q)
 
+    collect(1, KT // 4 - 1)
     for q in range(3):
         send_on(1, KT - 4 + q)
     pass_on(1, KT - 1)
 
     def add_up(p):
+        bulk(peers[p], chips - 1, chip_send.at[p], chip_recv.at[p]).wait_recv()
         total = part[p][dp]
         for o in range(1, chips):
             d = lax.rem(dp + chips - o, chips)
-            to_chip(p, d, d).wait_recv()
             total = total + peers[p][d]
         mine[p][...] = total
         for o in range(1, depth):
@@ -658,42 +666,32 @@
     out_gin = pltpu.make_async_copy(gin_ref, gin_hbm.at[0], out_sems.at[2])
     out_gin.start()
     add_up(1)
+    bulk(zparts_d, depth - 1, z_send.at[0], z_recv.at[0]).wait_recv()
     total = mine_d[pl.ds(pl.multiple_of(z * 8, 8), 8)]
     for o in range(1, depth):
         q = lax.rem(z + o, depth)
-        to_level(0, q, q).wait_recv()
         total = total + zparts_d[q]
     tot_d[pl.ds(pl.multiple_of(core * HALF_D + z * 8, 8), 8)] = total
     for o in range(1, size):
         gather_d(lax.rem(me + o, size), core, z).start()
+    bulk(zparts_x, depth - 1, z_send.at[1], z_recv.at[1]).wait_recv()
     total = mine_x[...]
     for o in range(1, depth):
         q = lax.rem(z + o, depth)
-        to_level(1, q, q).wait_recv()
         total = total + zparts_x[q]
     tot_x[half_of(1, core), :] = total
     last(core).start()
-    for o in range(1, size):
-        j = lax.rem(me + o, size)
-        gather_d(j, lax.rem(j, 2), j // 2).wait_recv()
+    bulk(tot_d, 8 * (size - 1), all_send.at[0], all_recv.at[0]).wait_recv()
     last(1 - core).wait_recv()
 
-    for o in range(1, size):
-        j = lax.rem(me + o, size)
-        there_h(j, me).wait_send()
-        there_a(j, me).wait_send()
-        home_h(j, me).wait_send()
-        home_a(j, me).wait_send()
+    for which, src in enumerate((send_h, send_a, back_h, back_a)):
+        bulk(src, size - 1, x_send.at[which], x_recv.at[0]).wait_send()
     last(core).wait_send()
-    for o in range(1, size):
-        gather_d(lax.rem(me + o, size), core, z).wait_send()
+    bulk(tot_d, 8 * (size - 1), all_send.at[0], all_recv.at[0]).wait_send()
     for p in range(2):
-        for d in range(chips):
-            to_sib(p, d).wait_send()
-        for o in range(1, chips):
-            to_chip(p, lax.rem(dp + o, chips), dp).wait_send()
-        for o in range(1, depth):
-            to_level(p, lax.rem(z + o, depth), z).wait_send()
+        bulk(pair[p], chips, pair_send.at[p], pair_recv.at[p, 0]).wait_send()
+        bulk(part[p], chips - 1, chip_send.at[p], chip_recv.at[p]).wait_send()
+        bulk(zparts[p], depth - 1, z_send.at[p], z_recv.at[p]).wait_send()
     out_gated.wait()
     out_ggate.wait()
     out_gin.wait()
@@ -765,9 +763,8 @@
             vm((HALF_D, 128)), vm((8, 8, 128)),
             vm((16, ROWS_X, 128)), vm((16, HALF_X, 128)), vm((16, HALF_X, 128)), vm((16, HALF_X, 128)),
             vm((HALF_X, 128)), vm((8, HALF_X, 128)),
-            dma((9,)), dma((3,)), dma((4, 16)), dma((4, 16)), dma((2, 16)), dma((2, 16)),
-            dma((2, 16)), dma((2, 16)), dma((2, 8)), dma((2, 8)), dma((1,)), dma((1,)),
-            dma((16,)), dma((16,)),
+            dma((9,)), dma((3,)), dma((4,)), dma((6,)), dma((2,)), dma((2, 8)),
+            dma((2,)), dma((2,)), dma((2,)), dma((2,)), dma((1,)), dma((1,)), dma((1,)), dma((1,)),
         ],
         compiler_params=pltpu.CompilerParams(
             collective_id=0, has_side_effects=True, vmem_limit_bytes=60 << 20

time: 73.6 us -> 70.7 us (0.961)
  Pallas kernels: 70.3 us -> 67.4 us
    pallas_call x1, Pallas kernels: 66.7 us -> 63.7 us  [call_step(): pl.pallas_call(step_kernel, out_shape=(big, big, big, sds((ROWS_D, 128)),...]
where the time goes in v4:
time: 70.7 us; the launch traced here: 69.4 us
  Pallas kernels  67.4 us (95%)
  between operations  1.95 us (3%)
    pallas_call x1, Pallas kernels, call_step(): pl.pallas_call(step_kernel, out_shape=(big, big, big, sds((ROWS_D, 128)),...  63.7 us
    pallas_call x1, Pallas kernels, call_finish(): pl.pallas_call(finish, out_shape=(big, big, big, sds((COLS, 128)), sds((R...  3.67 us

profile of v4, /device:TPU:1, one launch (start us, length us, event | category | flops | bytes accessed | tf_op | source)
XLA Modules:
  0.0 69.4 jit_solution(13506839541056242601)
XLA Ops:
  1.9 63.7 %step_kernel.1 = (bf16[1,128,2048]{2,1,0:T(8,128)(2,1)}, bf16[1,128,2048]{2,1,0:T(8,128)(2,1)}, bf16[1,128,2048]{2,1,0:T(8,128)(2,1)}, f32[128,128]{1,0:T(8,128)}, f32[64,128]{1,0:T(8,128)}) custom-call(s32[1]{0:T(128)S(6)} %copy.20.len_ref, s32[1]{0:T(128)S(6)} %copy.21.lab_ref, bf16[1,128,2048]{2,1,0:T(8,128)(2,1)} %u_hbm.1, ...), custom_call_target="tpu_custom_call" | custom-call | tf_op jit(solution)/shard_map/step_kernel/pallas_call | solution.py:744
  65.7 3.7 %finish.1 = (bf16[1,128,2048]{2,1,0:T(8,128)(2,1)}, bf16[1,128,2048]{2,1,0:T(8,128)(2,1)}, bf16[1,128,2048]{2,1,0:T(8,128)(2,1)}, f32[96,128]{1,0:T(8,128)}, f32...) custom-call(bf16[1,128,2048]{2,1,0:T(8,128)(2,1)} %get-tuple-element.23.gated, ...), custom_call_target="tpu_custom_call" | custom-call | tf_op jit(solution)/shard_map/finish/pallas_call | solution.py:778

commit v5 on v4

--- a/solution.py
+++ b/solution.py
@@ -698,10 +698,16 @@
 
 
 def finish(
-    gated_in, gin_in, ggate_in, tot_d, tot_x,
-    gated_out, gin_out, ggate_out, gx_ref, gdt_ref, ga_ref, gs_ref, gb_ref, gf_ref,
-    hold, in_sems, out_sems,
+    gated_in, gin_in, ggate_in, tot_d_in, tot_x_in,
+    gated_out, gin_out, ggate_out, gx_out, gdt_out, ga_out, gs_out, gb_out, gf_out,
+    hold, tot_d, tot_x, gx_ref, gdt_ref, ga_ref, gs_ref, gb_ref, gf_ref, in_sems, out_sems,
 ):
+    small = [
+        pltpu.make_async_copy(src, dst, in_sems.at[6 + i])
+        for i, (src, dst) in enumerate(((tot_d_in, tot_d), (tot_x_in, tot_x)))
+    ]
+    for copy in small:
+        copy.start()
     chunks = 2
     rows = T // chunks
     ins, outs = [], []
@@ -715,6 +721,8 @@
             outs.append(pltpu.make_async_copy(hold.at[i, at], dst.at[0, at], out_sems.at[one]))
     for copy in ins:
         copy.start()
+    for copy in small:
+        copy.wait()
     base = RANK + N
     gx_ref[0:RANK, :] = tot_x[...]
     gx_ref[RANK:COLS, :] = tot_d[base + 8 : base + 8 + 2 * N, :]
@@ -723,11 +731,22 @@
     gs_ref[...] = tot_d[base : base + 1, :]
     gb_ref[...] = tot_d[base + 1 : base + 2, :]
     gf_ref[...] = tot_d[base + 2 : base + 4, :]
+    last = [
+        pltpu.make_async_copy(src, dst, out_sems.at[6 + i])
+        for i, (src, dst) in enumerate(
+            (
+                (gx_ref, gx_out), (gdt_ref, gdt_out), (ga_ref, ga_out),
+                (gs_ref, gs_out), (gb_ref, gb_out), (gf_ref, gf_out),
+            )
+        )
+    ]
+    for copy in last:
+        copy.start()
     for into, out in zip(ins, outs):
         into.wait()
         out.start()
-    for out in outs:
-        out.wait()
+    for copy in last + outs:
+        copy.wait()
 
 
 def sds(shape, dtype=F32):
@@ -781,10 +800,12 @@
             big, big, big, sds((COLS, 128)), sds((RANK, 128)), sds((N, 128)), sds((1, 128)),
             sds((1, 128)), sds((2, 128)),
         ),
-        in_specs=[ANY, ANY, ANY, VMEM, VMEM],
-        out_specs=(ANY, ANY, ANY) + (VMEM,) * 6,
+        in_specs=[ANY] * 5,
+        out_specs=(ANY,) * 9,
         scratch_shapes=[
-            vm((3, T, E), BF16), pltpu.SemaphoreType.DMA((6,)), pltpu.SemaphoreType.DMA((6,)),
+            vm((3, T, E), BF16), vm((ROWS_D, 128)), vm((ROWS_X, 128)), vm((COLS, 128)), vm((RANK, 128)),
+            vm((N, 128)), vm((1, 128)), vm((1, 128)), vm((2, 128)),
+            pltpu.SemaphoreType.DMA((8,)), pltpu.SemaphoreType.DMA((12,)),
         ],
         name="finish",
     )(*operands)

time: 70.7 us -> 69.3 us (0.980)
  Pallas kernels: 67.4 us -> 66.1 us
    pallas_call x1, Pallas kernels: 3.67 us -> 2.32 us  [call_finish(): pl.pallas_call(finish, out_shape=(big, big, big, sds((COLS, 128)), sds((R...]
where the time goes in v5:
time: 69.3 us; the launch traced here: 68 us
  Pallas kernels  66.1 us (95%)
  between operations  1.95 us (3%)
    pallas_call x1, Pallas kernels, call_step(): pl.pallas_call(step_kernel, out_shape=(big, big, big, sds((ROWS_D, 128)),...  63.7 us
    pallas_call x1, Pallas kernels, call_finish(): pl.pallas_call(finish, out_shape=(big, big, big, sds((COLS, 128)), sds((R...  2.32 us

profile of v5, /device:TPU:1, one launch (start us, length us, event | category | flops | bytes accessed | tf_op | source)
XLA Modules:
  0.0 68.0 jit_solution(1513326716742449885)
XLA Ops:
  1.9 63.7 %step_kernel.1 = (bf16[1,128,2048]{2,1,0:T(8,128)(2,1)}, bf16[1,128,2048]{2,1,0:T(8,128)(2,1)}, bf16[1,128,2048]{2,1,0:T(8,128)(2,1)}, f32[128,128]{1,0:T(8,128)}, f32[64,128]{1,0:T(8,128)}) custom-call(s32[1]{0:T(128)S(6)} %copy.20.len_ref, s32[1]{0:T(128)S(6)} %copy.21.lab_ref, bf16[1,128,2048]{2,1,0:T(8,128)(2,1)} %u_hbm.1, ...), custom_call_target="tpu_custom_call" | custom-call | tf_op jit(solution)/shard_map/step_kernel/pallas_call | solution.py:763
  65.7 2.3 %finish.1 = (bf16[1,128,2048]{2,1,0:T(8,128)(2,1)}, bf16[1,128,2048]{2,1,0:T(8,128)(2,1)}, bf16[1,128,2048]{2,1,0:T(8,128)(2,1)}, f32[96,128]{1,0:T(8,128)}, f32...) custom-call(bf16[1,128,2048]{2,1,0:T(8,128)(2,1)} %get-tuple-element.23.gated, ...), custom_call_target="tpu_custom_call" | custom-call | tf_op jit(solution)/shard_map/finish/pallas_call | solution.py:797
